TPU v7x, 128 devices: a whole 4x4x4 slice. The times are simulated.
128 devices in a mesh: seq: 8 (over y, core), exp: 16 (over x, z).
Axes of the slice: x: 4, y: 4, z: 4, core: 2. Of those that a mesh axis runs over, the one named last changes fastest.
Arguments:
- moe_input: bfloat16 [1024, 4096], P('seq', 'exp'), may hold values from -6 to 6
- out_grad: bfloat16 [1024, 4096], P('seq', 'exp'), may hold values from -6 to 6
- expert_ids: int32 [1024, 2], P('seq'), may hold values from 0 to 7, all different within a row; in each aligned block of 128 rows (0 to 127, 128 to 255, ...) at most 48 rows name the same one
- expert_route_weights: float32 [1024, 2], P('seq'), may hold values from 0.1 to 1
- gate_weight: bfloat16 [16, 4096, 4096], P('exp', None, 'seq'), may hold values from -0.09375 to 0.09375
- up_weight: bfloat16 [16, 4096, 4096], P('exp', None, 'seq'), may hold values from -0.09375 to 0.09375
- down_weight: bfloat16 [16, 4096, 4096], P('exp', 'seq'), may hold values from -0.0625 to 0.0625
- out_weight: bfloat16 [8192, 4096], P(None, 'exp'), may hold values from -0.09375 to 0.09375
- scan_input: bfloat16 [8192, 1024], P('exp', 'seq'), may hold values from -6 to 6
- delta_raw: bfloat16 [8192, 1024], P('exp', 'seq'), may hold values from -1 to 1024
- mixer_gate_branch: bfloat16 [8192, 1024], P('exp', 'seq'), may hold values from -6 to 6
- state_input: float32 [16, 1024], P(None, 'seq'), may hold values from -0.25 to 0.25
- state_output: float32 [16, 1024], P(None, 'seq'), may hold values from -1.5 to 1.5
- log_rates: float32 [16, 8192], P(None, 'exp'), may hold values from -9 to -3
- skip_gain: float32 [8192], P('exp'), may hold values from 0.5 to 1.5
- block_states: float32 [8, 16, 8192], P('seq', None, 'exp'), may hold values from -6 to 6
Outputs:
- resid_grad: bfloat16 [1024, 4096], P('seq', 'exp')
- probs_grad: float32 [1024, 2], P('seq')
- input_grad: bfloat16 [8192, 1024], P('exp', 'seq')
- delta_grad: bfloat16 [8192, 1024], P('exp', 'seq')
- gate_grad: bfloat16 [8192, 1024], P('exp', 'seq')
- rates_grad: float32 [16, 8192], P(None, 'exp')
- skip_grad: float32 [8192], P('exp')
Inputs may be any that keep to these rules, and one draw needn't show every extreme that they name: `expert_ids`: within each aligned block of 128 rows (one sequence shard) no expert is named by more than 48 rows, and in every draw some expert is named by exactly 48 rows of some block.
All inputs are finite; a program needn't handle non-finite values.
Results may differ from a plain program's by a relative error of at most 0.0052.
Values may be sent and summed in bfloat16 or wider, within the bound.
A program may use at most 128 MiB of HBM per device.

v0:
```python
import jax
import jax.numpy as jnp
from jax import lax
from jax.experimental import pallas as pl
from jax.experimental.pallas import tpu as pltpu
from jax.sharding import PartitionSpec as P

N_SEQ = 8
F32 = jnp.float32
BF16 = jnp.bfloat16
VMEM = pl.BlockSpec(memory_space=pltpu.VMEM)
SMEM = pl.BlockSpec(memory_space=pltpu.SMEM)


def shape(dims, kind=jnp.float32):
    return jax.ShapeDtypeStruct(dims, kind)


LOG2E = 1.4426950408889634
GR = 4
TT = 128


def softplus(v):
    return jnp.maximum(v, 0.0) + jnp.log1p(jnp.exp(-jnp.abs(v)))


def sigmoid(v):
    return 1.0 / (1.0 + jnp.exp(-v))


def spread(ref, g, val):
    ref[pl.ds(g, TT, stride=8), :] = val
    ref[pl.ds(GR + g, TT, stride=8), :] = val


def column(rep, t):
    return jnp.take_along_axis(rep, jnp.full((8, 128), t, jnp.int32), axis=1)


def forward_kernel(u_ref, d_ref, b_ref, c_ref, lr_ref, st_ref, sk_ref, ear_ref, dt_ref, us_ref, so_ref):
    for g in range(GR):
        rows = pl.ds(g * 128, 128)
        spread(dt_ref, g, softplus(d_ref[rows, :].astype(jnp.float32).T))
        spread(us_ref, g, u_ref[rows, :].astype(jnp.float32).T)
    rate2 = [-LOG2E * jnp.exp(lr_ref[8 * j:8 * j + 8, :]) for j in range(8)]
    skip = sk_ref[...]

    def step(t, states):
        here = pl.ds(pl.multiple_of(t * 8, 8), 8)
        dt = dt_ref[here, :]
        u = us_ref[here, :]
        du = dt * u
        acc = jnp.zeros((8, 128), jnp.float32)
        out = []
        for j in range(8):
            ear_ref[pl.ds(pl.multiple_of(t * 64, 64) + 8 * j, 8), :] = states[j]
            b = column(b_ref[8 * j:8 * j + 8, :], t)
            c = column(c_ref[8 * j:8 * j + 8, :], t)
            state = jnp.exp2(dt * rate2[j]) * states[j] + du * b
            acc = acc + c * state
            out.append(state)
        so_ref[here, :] = acc + pltpu.roll(acc, 4, 0) + skip * u
        return tuple(out)

    lax.fori_loop(0, TT, step, tuple(st_ref[8 * j:8 * j + 8, :] for j in range(8)), unroll=2)


def middle_kernel(in_ref, z_ref, c_ref, lr_ref, dt_ref, so_ref, y_ref, gate_ref, pair_ref):
    for g in range(GR):
        rows = pl.ds(g * 128, 128)
        up = in_ref[rows, :]
        z = z_ref[rows, :].astype(jnp.float32)
        sig = sigmoid(z)
        spread(y_ref, g, (up * z * sig).T)
        so = so_ref[pl.ds(g, TT, stride=8), :].T
        gate_ref[rows, :] = (up * so * sig * (1.0 + z * (1.0 - sig))).astype(jnp.bfloat16)
    rate2 = [-LOG2E * jnp.exp(lr_ref[8 * j:8 * j + 8, :]) for j in range(8)]

    def step(i, carry):
        t = TT - 1 - i
        here = pl.ds(pl.multiple_of(t * 8, 8), 8)
        dt = dt_ref[here, :]
        y = y_ref[here, :]
        total = carry[8] + dt
        out = []
        for j in range(8):
            c = column(c_ref[8 * j:8 * j + 8, :], t)
            out.append(jnp.exp2(dt * rate2[j]) * (c * y + carry[j]))
        return tuple(out) + (total,)

    zero = jnp.zeros((8, 128), jnp.float32)
    last = lax.fori_loop(0, TT, step, (zero,) * 9, unroll=2)
    for j in range(8):
        pair_ref[8 * j:8 * j + 8, :] = last[j]
        pair_ref[64 + 8 * j:72 + 8 * j, :] = jnp.exp2(rate2[j] * last[8])


def final_kernel(me_ref, all_ref, y_ref, ear_ref, dt_ref, us_ref, d_ref, b_ref, c_ref, lr_ref, sk_ref,
                 input_ref, delta_ref, part_ref, s1_ref, dl_ref):
    me = me_ref[0]
    rate = [jnp.exp(lr_ref[8 * j:8 * j + 8, :]) for j in range(8)]
    rate2 = [-LOG2E * rate[j] for j in range(8)]
    start = []
    for j in range(8):
        inc = jnp.zeros((8, 128), jnp.float32)
        for r in range(N_SEQ - 1, 0, -1):
            term = all_ref[r, 8 * j:8 * j + 8, :]
            decay = all_ref[r, 64 + 8 * j:72 + 8 * j, :]
            inc = jnp.where(r > me, term + decay * inc, inc)
        start.append(inc)

    def step(i, carry):
        vs, sums, sk = carry
        t = TT - 1 - i
        here = pl.ds(pl.multiple_of(t * 8, 8), 8)
        dt = dt_ref[here, :]
        y = y_ref[here, :]
        s1 = jnp.zeros((8, 128), jnp.float32)
        dl = jnp.zeros((8, 128), jnp.float32)
        nv, ns = [], []
        for j in range(8):
            b = column(b_ref[8 * j:8 * j + 8, :], t)
            c = column(c_ref[8 * j:8 * j + 8, :], t)
            adj = c * y + vs[j]
            v = jnp.exp2(dt * rate2[j]) * adj
            x = v * ear_ref[pl.ds(pl.multiple_of(t * 64, 64) + 8 * j, 8), :]
            s1 = s1 + adj * b
            dl = dl + rate[j] * x
            ns.append(sums[j] + dt * x)
            nv.append(v)
        s1_ref[here, :] = s1 + pltpu.roll(s1, 4, 0)
        dl_ref[here, :] = dl + pltpu.roll(dl, 4, 0)
        return tuple(nv), tuple(ns), sk + y * us_ref[here, :]

    zero = jnp.zeros((8, 128), jnp.float32)
    vs, sums, sk = lax.fori_loop(0, TT, step, (tuple(start), (zero,) * 8, zero), unroll=2)
    for j in range(8):
        part_ref[8 * j:8 * j + 8, :] = -rate[j] * sums[j]
    part_ref[64:72, :] = sk
    for g in range(GR):
        rows = pl.ds(g * 128, 128)
        mine = pl.ds(g, TT, stride=8)
        s1 = s1_ref[mine, :]
        inp = s1 * dt_ref[mine, :] + sk_ref[g:g + 1, :] * y_ref[mine, :]
        input_ref[rows, :] = inp.T.astype(jnp.bfloat16)
        step_grad = us_ref[mine, :] * s1 - dl_ref[mine, :]
        delta_ref[rows, :] = (step_grad.T * sigmoid(d_ref[rows, :].astype(jnp.float32))).astype(jnp.bfloat16)


def expert_backward(rows_in, rows_grad, gate_slice, up_slice, down_slice):
    contract = (((1,), (1,)), ((), ()))
    gate_pre = jnp.dot(rows_in, gate_slice, preferred_element_type=jnp.float32)
    up_pre = jnp.dot(rows_in, up_slice, preferred_element_type=jnp.float32)
    hidden_grad = lax.dot_general(
        rows_grad, down_slice, contract, preferred_element_type=jnp.float32
    )
    gate_sig = jax.nn.sigmoid(gate_pre)
    silu_gate = gate_pre * gate_sig
    probes = jnp.sum(silu_gate * up_pre * hidden_grad, axis=1)
    grad_up = (hidden_grad * silu_gate).astype(jnp.bfloat16)
    grad_gate = (hidden_grad * up_pre * gate_sig * (1.0 + gate_pre * (1.0 - gate_sig))).astype(
        jnp.bfloat16
    )
    partial_rows = lax.dot_general(
        grad_gate, gate_slice, contract, preferred_element_type=jnp.float32
    )
    partial_rows = partial_rows + lax.dot_general(
        grad_up, up_slice, contract, preferred_element_type=jnp.float32
    )
    return (partial_rows, probes)


def local(
    moe_input,
    out_grad,
    expert_ids,
    expert_route_weights,
    gate_weight,
    up_weight,
    down_weight,
    out_weight,
    scan_input,
    delta_raw,
    mixer_gate_branch,
    state_input,
    state_output,
    log_rates,
    skip_gain,
    block_states,
):
    seq_count = lax.axis_size("seq")
    exp_count = lax.axis_size("exp")
    row_count, feat_cols = moe_input.shape
    top_count = expert_ids.shape[1]
    experts = exp_count // 2
    capacity = 3 * top_count * row_count // (2 * experts)
    b_rep = jnp.repeat(state_input, GR, axis=0)
    c_rep = jnp.repeat(state_output, GR, axis=0)
    rates = log_rates.reshape(64, 128)
    start = block_states.reshape(64, 128)
    skip = jnp.tile(skip_gain.reshape(GR, 128), (2, 1))
    earlier, steps, signal, scan_out = pl.pallas_call(
        forward_kernel,
        out_shape=(shape((TT * 64, 128)), shape((TT * 8, 128)), shape((TT * 8, 128)), shape((TT * 8, 128))),
        in_specs=[VMEM] * 7,
        out_specs=(VMEM,) * 4,
        name="scan_forward",
    )(scan_input, delta_raw, b_rep, c_rep, rates, start, skip)
    flat_ids = expert_ids.reshape(row_count * top_count)
    matches = (flat_ids[:, None] == jnp.arange(experts, dtype=jnp.int32)[None, :]).astype(jnp.int32)
    slot_ids = jnp.sum((jnp.cumsum(matches, axis=0) - matches) * matches, axis=1)
    owners = jnp.arange(row_count * top_count, dtype=jnp.int32) // top_count
    slot_table = jnp.zeros((capacity, experts), jnp.int32).at[slot_ids, flat_ids].set(owners)
    send_in = moe_input[slot_table]
    send_grad = out_grad[slot_table]

    def widen_all(block):
        wide = jnp.broadcast_to(
            block[:, None, :, None, :], (capacity, seq_count, experts, 2, feat_cols)
        )
        return wide.reshape(capacity, seq_count * exp_count, feat_cols)

    got_in, got_grad = (
        lax.all_to_all(widen_all(send_in), ("seq", "exp"), split_axis=1, concat_axis=1, tiled=True),
        lax.all_to_all(
            widen_all(send_grad), ("seq", "exp"), split_axis=1, concat_axis=1, tiled=True
        ),
    )
    rows_in = got_in.reshape(capacity * seq_count, exp_count * feat_cols)
    rows_grad = got_grad.reshape(capacity * seq_count, exp_count * feat_cols)
    partial_rows, probes = expert_backward(
        rows_in, rows_grad, gate_weight[0], up_weight[0], down_weight[0]
    )
    part_back = partial_rows.reshape(capacity, seq_count * exp_count, feat_cols)
    probe_back = jnp.broadcast_to(
        probes.reshape(capacity, seq_count, 1, 1), (capacity, seq_count, exp_count, 1)
    ).reshape(capacity, seq_count * exp_count, 1)
    back_part, back_probe = (
        lax.all_to_all(part_back, ("seq", "exp"), split_axis=1, concat_axis=1, tiled=True),
        lax.all_to_all(probe_back, ("seq", "exp"), split_axis=1, concat_axis=1, tiled=True),
    )
    route_sum = jnp.sum(back_part.reshape(capacity, seq_count, experts, 2, feat_cols), axis=(1, 3))
    probe_sum = jnp.sum(back_probe.reshape(capacity, seq_count, experts, 2), axis=(1, 3))
    route_grad = route_sum[slot_ids, flat_ids].reshape(row_count, top_count, feat_cols)
    probs_grad = probe_sum[slot_ids, flat_ids].reshape(row_count, top_count)
    mixture = jnp.sum(expert_route_weights[:, :, None] * route_grad, axis=1)
    resid_grad = (out_grad.astype(jnp.float32) + mixture).astype(jnp.bfloat16)
    block = out_weight
    inner_grad = lax.psum_scatter(
        lax.dot_general(
            block, resid_grad, (((1,), (1,)), ((), ())), preferred_element_type=jnp.float32
        ),
        "exp",
        scatter_dimension=0,
        tiled=True,
    )
    y_grad, gate_grad, pair = pl.pallas_call(
        middle_kernel,
        out_shape=(shape((TT * 8, 128)), shape((512, 128), BF16), shape((128, 128))),
        in_specs=[VMEM] * 6,
        out_specs=(VMEM,) * 3,
        name="adjoint_summary",
    )(inner_grad, mixer_gate_branch, c_rep, rates, steps, scan_out)
    pairs = lax.all_gather(pair, "seq")
    me = lax.axis_index("seq").astype(jnp.int32).reshape(1)
    input_grad, delta_grad, part = pl.pallas_call(
        final_kernel,
        out_shape=(shape((512, 128), BF16), shape((512, 128), BF16), shape((72, 128))),
        in_specs=[SMEM] + [VMEM] * 10,
        out_specs=(VMEM,) * 3,
        scratch_shapes=[pltpu.VMEM((TT * 8, 128), F32)] * 2,
        name="adjoint_final",
    )(me, pairs, y_grad, earlier, steps, signal, delta_raw, b_rep, c_rep, rates, skip)
    total = lax.psum(part, "seq")
    rates_grad = total[:64].reshape(16, 512)
    skip_grad = total[64:68].reshape(512)
    return (resid_grad, probs_grad, input_grad, delta_grad, gate_grad, rates_grad, skip_grad)


def solution(mesh):
    in_specs = (
        P("seq", "exp"),
        P("seq", "exp"),
        P("seq", None),
        P("seq", None),
        P("exp", None, "seq"),
        P("exp", None, "seq"),
        P("exp", "seq", None),
        P(None, "exp"),
        P("exp", "seq"),
        P("exp", "seq"),
        P("exp", "seq"),
        P(None, "seq"),
        P(None, "seq"),
        P(None, "exp"),
        P("exp"),
        P("seq", None, "exp"),
    )
    out_specs = (
        P("seq", "exp"),
        P("seq", None),
        P("exp", "seq"),
        P("exp", "seq"),
        P("exp", "seq"),
        P(None, "exp"),
        P("exp"),
    )
    return jax.shard_map(local, mesh=mesh, in_specs=in_specs, out_specs=out_specs, check_vma=False)
```

profile of v0, /device:TPU:1, one launch (start us, length us, event | category | flops | bytes accessed | tf_op | source)
XLA Modules:
  0.0 396.0 jit_solution(10216028105053342441)
XLA Ops:
  9.4 11.3 %scatter_fusion = s32[48,8]{0,1:T(8,128)S(1)} fusion(s32[48,8]{0,1:T(8,128)S(1)} %broadcast.77, s32[256]{0:T(256)S(1)} %bitcast.52, s32[256]{0:T(256)S(1)} %and_select_fusion), kind=kCustom, calls=%fused_computation.4 | custom fusion | bytes 5120 | tf_op jit(solution)/shard_map/scatter | solution.py:214
  25.0 11.5 %all-to-all-start.1 = ((bf16[48,128,256]{2,0,1:T(8,128)(2,1)}), bf16[48,128,256]{2,0,1:T(8,128)(2,1)S(1)}, u32[]{:S(2)}, u32[]{:S(2)}) async-start(bf16[48,128,256]{2,0,1:T(8,128)(2,1)} %bitcast.54), calls=%async_computation.1 | async-start | bytes 6291456 | tf_op jit(solution)/shard_map/all_to_all | solution.py:225
  40.0 37.4 %all-to-all-done.1 = bf16[48,128,256]{2,0,1:T(8,128)(2,1)S(1)} async-done(((bf16[48,128,256]{2,0,1:T(8,128)(2,1)}), bf16[48,128,256]{2,0,1:T(8,128)(2,1)S(1)}, u32[]{:S(2)}, u32[]{:S(2)}) %all-to-all-start.1) | async-done | bytes 3145760 | tf_op jit(solution)/shard_map/all_to_all | solution.py:225
  79.5 5.3 %all-to-all-start = ((bf16[48,128,256]{2,0,1:T(8,128)(2,1)}), bf16[48,128,256]{2,0,1:T(8,128)(2,1)}, u32[]{:S(2)}, u32[]{:S(2)}) async-start(bf16[48,128,256]{2,0,1:T(8,128)(2,1)} %bitcast.53), calls=%async_computation | async-start | bytes 6291456 | tf_op jit(solution)/shard_map/all_to_all | solution.py:226
  87.6 4.2 %reshape.143 = bf16[384,4096]{1,0:T(8,128)(2,1)S(1)} reshape(bf16[48,128,256]{2,1,0:T(8,128)(2,1)} %copy.68) | data formatting | bytes 6291456 | tf_op jit(solution)/shard_map/reshape | solution.py:230
  91.8 5.1 %fusion.2 = f32[384,512]{1,0:T(8,128)} fusion(bf16[384,4096]{1,0:T(8,128)(2,1)S(1)} %reshape.143, bf16[1,4096,512]{2,1,0:T(8,128)(2,1)} %param.20), kind=kOutput, calls=%fused_computation.9 | convolution fusion | flops 1610612736 | bytes 8126464 | tf_op jit(solution)/shard_map/dot_general | solution.py:153
  99.6 25.9 %all-to-all-done = bf16[48,128,256]{2,0,1:T(8,128)(2,1)} async-done(((bf16[48,128,256]{2,0,1:T(8,128)(2,1)}), bf16[48,128,256]{2,0,1:T(8,128)(2,1)}, u32[]{:S(2)}, u32[]{:S(2)}) %all-to-all-start) | async-done | bytes 3145760 | tf_op jit(solution)/shard_map/all_to_all | solution.py:226
  125.5 3.0 copy.66
  128.5 3.4 reshape.141
  131.9 5.6 %multiply_reduce_fusion = (f32[384]{0:T(512)S(1)}, f32[384,512]{1,0:T(8,128)S(1)}) fusion(f32[384,512]{1,0:T(8,128)} %fusion.5, f32[384,512]{1,0:T(8,128)} %fusion.2, bf16[384,4096]{1,0:T(8,128)(2,1)} %reshape.141, bf16[1,512,4096]{2,1,0:T(8,128)(2,1)} %param.22), kind=kOutput, calls=%fused_computation.16 | convolution fusion | flops 1611988608 | bytes 9700864 | tf_op jit(solution)/shard_map/dot_general | solution.py:155
  139.8 4.5 %convolution_add_fusion = f32[384,4096]{1,0:T(8,128)} fusion(f32[384,4096]{1,0:T(8,128)S(1)} %fusion, bf16[1,4096,512]{2,1,0:T(8,128)(2,1)S(1)} %copy-done.6, f32[384,512]{1,0:T(8,128)S(1)} %get-tuple-element.58, f32[384,512]{1,0:T(8,128)S(1)} %copy-done.3), kind=kOutput, calls=%fused_computation.6 | convolution fusion | flops 1613365248 | bytes 18350080 | tf_op jit(solution)/shard_map/dot_general | solution.py:168
  144.3 7.1 %reshape.144 = f32[48,128,256]{2,1,0:T(8,128)} reshape(f32[384,4096]{1,0:T(8,128)} %convolution_add_fusion) | data formatting | bytes 12582912 | tf_op jit(solution)/shard_map/reshape | solution.py:235
  151.4 9.1 %copy.69 = f32[48,128,256]{2,0,1:T(8,128)} copy(f32[48,128,256]{2,1,0:T(8,128)} %reshape.144) | data formatting | bytes 12582912 | tf_op jit(solution)/shard_map/reshape | solution.py:235
  160.5 5.5 %all-to-all-start.2 = ((f32[48,128,256]{2,0,1:T(8,128)}), f32[48,128,256]{2,0,1:T(8,128)}, u32[]{:S(2)}, u32[]{:S(2)}) async-start(f32[48,128,256]{2,0,1:T(8,128)} %copy.69), calls=%async_computation.2 | async-start | bytes 12582912 | tf_op jit(solution)/shard_map/all_to_all | solution.py:240
  166.2 75.5 %all-to-all-done.2 = f32[48,128,256]{2,0,1:T(8,128)} async-done(((f32[48,128,256]{2,0,1:T(8,128)}), f32[48,128,256]{2,0,1:T(8,128)}, u32[]{:S(2)}, u32[]{:S(2)}) %all-to-all-start.2) | async-done | bytes 6291488 | tf_op jit(solution)/shard_map/all_to_all | solution.py:240
  241.6 3.3 reduce_sum.49
  247.1 5.4 %convolution_bitcast_fusion = f32[8192,128]{1,0:T(8,128)} fusion(bf16[128,256]{1,0:T(8,128)(2,1)S(1)} %add_convert_fusion, bf16[8192,256]{1,0:T(8,128)(2,1)} %param.23), kind=kOutput, calls=%fused_computation.5 | convolution fusion | flops 536870912 | bytes 8454144 | tf_op jit(solution)/shard_map/dot_general | solution.py:251
  253.4 5.6 %all-to-all-start.3 = ((f32[48,128,1]{0,2,1:T(1,128)}), f32[48,128,1]{0,2,1:T(1,128)S(1)}, u32[]{:S(2)}, u32[]{:S(2)}) async-start(f32[48,128,1]{0,2,1:T(1,128)} %bitcast.14), calls=%async_computation.3 | async-start | bytes 131072 | tf_op jit(solution)/shard_map/all_to_all | solution.py:241
  262.1 11.7 %scan_forward.1 = (f32[8192,128]{1,0:T(8,128)}, f32[1024,128]{1,0:T(8,128)}, f32[1024,128]{1,0:T(8,128)}, f32[1024,128]{1,0:T(8,128)}) custom-call(bf16[512,128]{1,0:T(8,128)(2,1)} %u_ref.1, bf16[512,128]{1,0:T(8,128)(2,1)} %d_ref.3, f32[64,128]{1,0:T(8,128)} %bitcast.61, f32[64,128]{1,0:T(8,128)} %bitcast.58, f32[64,128]{1,0:T(8,128)} %reshape.151.lr_ref, ...), custom_call_target="tpu_custom_call" | custom-call | tf_op jit(solution)/shard_map/scan_forward/pallas_call | solution.py:203
  276.1 51.4 %reduce-scatter.2.cloned.1.call-done.in_ref = f32[512,128]{1,0:T(8,128)} async-done(((f32[8192,128]{1,0:T(8,128)}), f32[512,128]{1,0:T(8,128)}) %reduce-scatter.2.cloned.1.call-update) | async-done | bytes 262160 | tf_op jit(solution)/shard_map/reduce_scatter | solution.py:250
  327.4 8.4 %adjoint_summary.1 = (f32[1024,128]{1,0:T(8,128)}, bf16[512,128]{1,0:T(8,128)(2,1)}, f32[128,128]{1,0:T(8,128)}) custom-call(f32[512,128]{1,0:T(8,128)} %reduce-scatter.2.cloned.1.call-done.in_ref, bf16[512,128]{1,0:T(8,128)(2,1)} %z_ref.1, f32[64,128]{1,0:T(8,128)} %bitcast.59, f32[64,128]{1,0:T(8,128)} %reshape.151.lr_ref, ...), custom_call_target="tpu_custom_call" | custom-call | tf_op jit(solution)/shard_map/adjoint_summary/pallas_call | solution.py:258
  335.8 17.0 %all-gather = f32[1024,128]{1,0:T(8,128)} all-gather(f32[128,128]{1,0:T(8,128)} %get-tuple-element.19), channel_id=2, replica_groups=mesh['seq'=8,'exp'=16] {'seq'}, dimensions={0}, use_global_device_ids=true | all-gather | bytes 589824 | tf_op jit(solution)/shard_map/all_gather | solution.py:265
  352.8 11.7 %adjoint_final.1 = (bf16[512,128]{1,0:T(8,128)(2,1)}, bf16[512,128]{1,0:T(8,128)(2,1)}, f32[72,128]{1,0:T(8,128)}) custom-call(s32[1]{0:T(128)} %bitcast.16.me_ref, f32[8,128,128]{2,1,0:T(8,128)} %bitcast.55, f32[1024,128]{1,0:T(8,128)} %get-tuple-element.20.y_ref, f32[8192,128]{1,0:T(8,128)} %get-tuple-element.21.ear_ref, ...), custom_call_target="tpu_custom_call" | custom-call | tf_op jit(solution)/shard_map/adjoint_final/pallas_call | solution.py:267
  364.6 23.4 %psum.7 = f32[72,128]{1,0:T(8,128)S(1)} all-reduce(f32[72,128]{1,0:T(8,128)} %get-tuple-element.26), channel_id=1, replica_groups=mesh['seq'=8,'exp'=16] {'seq'}, use_global_device_ids=true, to_apply=%region_9.10 | all-reduce | flops 9216 | bytes 73728 | tf_op jit(solution)/shard_map/psum | solution.py:275
  (80 shorter events, 29.3 us)
Async XLA Ops:
  7.2 13.8 %copy-start = (bf16[128,256]{1,0:T(8,128)(2,1)S(1)}, bf16[128,256]{1,0:T(8,128)(2,1)}, u32[]{:S(2)}) copy-start(bf16[128,256]{1,0:T(8,128)(2,1)} %param.16) | copy-start | bytes 196612
  23.1 13.5 %copy-start.2 = (bf16[128,256]{1,0:T(8,128)(2,1)S(1)}, bf16[128,256]{1,0:T(8,128)(2,1)}, u32[]{:S(2)}) copy-start(bf16[128,256]{1,0:T(8,128)(2,1)} %param.17) | copy-start | bytes 196612
  25.0 52.4 %all-to-all-start.1 = ((bf16[48,128,256]{2,0,1:T(8,128)(2,1)}), bf16[48,128,256]{2,0,1:T(8,128)(2,1)S(1)}, u32[]{:S(2)}, u32[]{:S(2)}) async-start(bf16[48,128,256]{2,0,1:T(8,128)(2,1)} %bitcast.54), calls=%async_computation.1 | async-start | bytes 6291456 | tf_op jit(solution)/shard_map/all_to_all | solution.py:225
  79.5 46.1 %all-to-all-start = ((bf16[48,128,256]{2,0,1:T(8,128)(2,1)}), bf16[48,128,256]{2,0,1:T(8,128)(2,1)}, u32[]{:S(2)}, u32[]{:S(2)}) async-start(bf16[48,128,256]{2,0,1:T(8,128)(2,1)} %bitcast.53), calls=%async_computation | async-start | bytes 6291456 | tf_op jit(solution)/shard_map/all_to_all | solution.py:226
  91.8 5.1 %copy-start.5 = (bf16[1,4096,512]{2,1,0:T(8,128)(2,1)S(1)}, bf16[1,4096,512]{2,1,0:T(8,128)(2,1)}, u32[]{:S(2)}) copy-start(bf16[1,4096,512]{2,1,0:T(8,128)(2,1)} %param.21) | copy-start | bytes 12582916
  131.9 5.6 %copy-start.3 = (f32[384,512]{1,0:T(8,128)S(1)}, f32[384,512]{1,0:T(8,128)}, u32[]{:S(2)}) copy-start(f32[384,512]{1,0:T(8,128)} %fusion.2) | copy-start | bytes 2359300
  131.9 5.6 %copy-start.4 = (bf16[1,4096,512]{2,1,0:T(8,128)(2,1)S(1)}, bf16[1,4096,512]{2,1,0:T(8,128)(2,1)}, u32[]{:S(2)}) copy-start(bf16[1,4096,512]{2,1,0:T(8,128)(2,1)} %param.20) | copy-start | bytes 12582916
  131.9 5.7 %copy-start.7 = (f32[384,512]{1,0:T(8,128)S(1)}, f32[384,512]{1,0:T(8,128)}, u32[]{:S(2)}) copy-start(f32[384,512]{1,0:T(8,128)} %fusion.5) | copy-start | bytes 2359300
  137.6 2.2 copy-start.6
  160.5 5.6 %copy-start.14 = (f32[128,2]{0,1:T(2,128)S(1)}, f32[128,2]{0,1:T(2,128)}, u32[]{:S(2)}) copy-start(f32[128,2]{0,1:T(2,128)} %param.19) | copy-start | bytes 3076
  160.5 81.1 %all-to-all-start.2 = ((f32[48,128,256]{2,0,1:T(8,128)}), f32[48,128,256]{2,0,1:T(8,128)}, u32[]{:S(2)}, u32[]{:S(2)}) async-start(f32[48,128,256]{2,0,1:T(8,128)} %copy.69), calls=%async_computation.2 | async-start | bytes 12582912 | tf_op jit(solution)/shard_map/all_to_all | solution.py:240
  166.0 161.4 %reduce-scatter.2.cloned.1.call-start = ((), (), s32[]{:S(2)}) async-start(), calls=%async_computation.5 | async-start | bytes 4456448 | tf_op jit(solution)/shard_map/reduce_scatter | solution.py:250
  247.1 5.4 %copy-start.8 = (bf16[128,256]{1,0:T(8,128)(2,1)}, bf16[128,256]{1,0:T(8,128)(2,1)S(1)}, u32[]{:S(2)}) copy-start(bf16[128,256]{1,0:T(8,128)(2,1)S(1)} %add_convert_fusion) | copy-start | bytes 196612
  252.6 6.5 %copy-start.9 = (f32[16,512]{1,0:T(8,128)S(1)}, f32[16,512]{1,0:T(8,128)}, u32[]{:S(2)}) copy-start(f32[16,512]{1,0:T(8,128)} %param.29) | copy-start | bytes 98308
  252.6 7.1 %copy-start.10 = (f32[1,16,512]{2,1,0:T(8,128)S(1)}, f32[1,16,512]{2,1,0:T(8,128)}, u32[]{:S(2)}) copy-start(f32[1,16,512]{2,1,0:T(8,128)} %param.31) | copy-start | bytes 98308
  252.6 7.7 %copy-start.11 = (f32[16,128]{1,0:T(8,128)S(1)}, f32[16,128]{1,0:T(8,128)}, u32[]{:S(2)}) copy-start(f32[16,128]{1,0:T(8,128)} %param.28) | copy-start | bytes 24580
  252.6 8.4 %copy-start.12 = (f32[16,128]{1,0:T(8,128)S(1)}, f32[16,128]{1,0:T(8,128)}, u32[]{:S(2)}) copy-start(f32[16,128]{1,0:T(8,128)} %param.27) | copy-start | bytes 24580
  252.6 9.0 %copy-start.13 = (f32[512]{0:T(512)S(1)}, f32[512]{0:T(512)}, u32[]{:S(2)}) copy-start(f32[512]{0:T(512)} %param.30) | copy-start | bytes 6148
  253.4 20.4 %all-to-all-start.3 = ((f32[48,128,1]{0,2,1:T(1,128)}), f32[48,128,1]{0,2,1:T(1,128)S(1)}, u32[]{:S(2)}, u32[]{:S(2)}) async-start(f32[48,128,1]{0,2,1:T(1,128)} %bitcast.14), calls=%async_computation.3 | async-start | bytes 131072 | tf_op jit(solution)/shard_map/all_to_all | solution.py:241
  327.4 61.7 %copy-start.1 = (bf16[128,256]{1,0:T(8,128)(2,1)S(1)}, bf16[128,256]{1,0:T(8,128)(2,1)}, u32[]{:S(2)}) copy-start(bf16[128,256]{1,0:T(8,128)(2,1)} %param.16) | copy-start | bytes 196612
Sparse Core Ops, SparseCore 0:
  252.7 74.6 reduce-scatter.1
where the time goes:
time: 399 us; the launch traced here: 396 us
  waiting for transfers between devices  190 us (48%)
  local copies, waits for them, and re-layouts  61.5 us (15%)
  blocking collectives  40.4 us (10%)
  Pallas kernels  31.8 us (8%)
  starting transfers between devices  27.9 us (7%)
  matrix products  25.3 us (6%)
  between operations  14.4 us (4%)
  other arithmetic  4.46 us (1%)
    all_to_all x1, waiting for transfers between devices, local(): lax.all_to_all(part_back, ('seq', 'exp'), split_axis=1, concat_axis=1, ti...  75.5 us
    reduce_scatter x1, waiting for transfers between devices, local(): lax.psum_scatter(lax.dot_general(block, resid_grad, (((1,), (1,)), ((), (...  51.4 us
    all_to_all x1, waiting for transfers between devices, local(): lax.all_to_all(widen_all(send_in), ('seq', 'exp'), split_axis=1, concat_a...  37.4 us
    all_to_all x1, waiting for transfers between devices, local(): lax.all_to_all(widen_all(send_grad), ('seq', 'exp'), split_axis=1, concat...  25.9 us
    psum x1, blocking collectives, local(): total = lax.psum(part, 'seq')  23.4 us
    all_gather x1, blocking collectives, local(): pairs = lax.all_gather(pair, 'seq')  17 us
    reshape x2, local copies, waits for them, and re-layouts, local(): part_back = partial_rows.reshape(capacity, seq_count * exp_count, feat_cols)  16.2 us
    pallas_call x1, Pallas kernels, local(): pl.pallas_call(final_kernel, out_shape=(shape((512, 128), BF16), shape((5...  11.7 us
  transfers between devices with their start and end apart: 5, of which 4 were waited for; matrix products, arithmetic and copies ran while one was open for 6% of the time, Pallas kernels for 3%

commit v1 on v0

--- a/solution.py
+++ b/solution.py
@@ -69,12 +69,12 @@
 def middle_kernel(in_ref, z_ref, c_ref, lr_ref, dt_ref, so_ref, y_ref, gate_ref, pair_ref):
     for g in range(GR):
         rows = pl.ds(g * 128, 128)
-        up = in_ref[rows, :]
-        z = z_ref[rows, :].astype(jnp.float32)
+        up = in_ref[:, rows]
+        z = z_ref[rows, :].astype(jnp.float32).T
         sig = sigmoid(z)
-        spread(y_ref, g, (up * z * sig).T)
-        so = so_ref[pl.ds(g, TT, stride=8), :].T
-        gate_ref[rows, :] = (up * so * sig * (1.0 + z * (1.0 - sig))).astype(jnp.bfloat16)
+        spread(y_ref, g, up * z * sig)
+        so = so_ref[pl.ds(g, TT, stride=8), :]
+        gate_ref[rows, :] = (up * so * sig * (1.0 + z * (1.0 - sig))).T.astype(jnp.bfloat16)
     rate2 = [-LOG2E * jnp.exp(lr_ref[8 * j:8 * j + 8, :]) for j in range(8)]
 
     def step(i, carry):
@@ -148,27 +148,343 @@
         delta_ref[rows, :] = (step_grad.T * sigmoid(d_ref[rows, :].astype(jnp.float32))).astype(jnp.bfloat16)
 
 
-def expert_backward(rows_in, rows_grad, gate_slice, up_slice, down_slice):
-    contract = (((1,), (1,)), ((), ()))
-    gate_pre = jnp.dot(rows_in, gate_slice, preferred_element_type=jnp.float32)
-    up_pre = jnp.dot(rows_in, up_slice, preferred_element_type=jnp.float32)
-    hidden_grad = lax.dot_general(
-        rows_grad, down_slice, contract, preferred_element_type=jnp.float32
-    )
-    gate_sig = jax.nn.sigmoid(gate_pre)
-    silu_gate = gate_pre * gate_sig
-    probes = jnp.sum(silu_gate * up_pre * hidden_grad, axis=1)
-    grad_up = (hidden_grad * silu_gate).astype(jnp.bfloat16)
-    grad_gate = (hidden_grad * up_pre * gate_sig * (1.0 + gate_pre * (1.0 - gate_sig))).astype(
-        jnp.bfloat16
-    )
-    partial_rows = lax.dot_general(
-        grad_gate, gate_slice, contract, preferred_element_type=jnp.float32
-    )
-    partial_rows = partial_rows + lax.dot_general(
-        grad_up, up_slice, contract, preferred_element_type=jnp.float32
-    )
-    return (partial_rows, probes)
+MESH = pl.DeviceIdType.MESH
+ANY = pl.BlockSpec(memory_space=pl.ANY)
+CAP = 48
+
+
+def places():
+    q = lax.axis_index("seq")
+    e = lax.axis_index("exp")
+    return q, e
+
+
+def greet(peers):
+    barrier = pltpu.get_barrier_semaphore()
+    for peer in peers:
+        pl.semaphore_signal(barrier, inc=1, device_id=peer, device_id_type=MESH)
+    pl.semaphore_wait(barrier, len(peers))
+
+
+class Copies:
+    def __init__(self, send, recv):
+        self.send, self.recv, self.all, self.next = send, recv, [], 0
+
+    def start(self, src, dst, peer):
+        n = self.next
+        self.next = n + 1
+        copy = pltpu.make_async_remote_copy(
+            src_ref=src, dst_ref=dst, send_sem=self.send.at[n], recv_sem=self.recv.at[n],
+            device_id=peer, device_id_type=MESH,
+        )
+        copy.start()
+        self.all.append(copy)
+        return copy
+
+    def finish(self):
+        for copy in self.all:
+            copy.wait_send()
+
+
+def seq_at(y, c):
+    return lax.rem(y + 4, 4) * 2 + c
+
+
+def dispatch_kernel(s_ref, r_ref, send, recv, own_sem):
+    q, e = places()
+    y, c = q // 2, lax.rem(q, 2)
+    qu, qd, q2, qc = seq_at(y + 1, c), seq_at(y - 1, c), seq_at(y + 2, c), y * 2 + 1 - c
+    far = [(q, lax.rem(e + k, 16)) for k in range(1, 16)]
+    up, down, core = (qu, e), (qd, e), (qc, e)
+    greet(far + [up, down, core])
+    cp = Copies(send, recv)
+    own = pltpu.make_async_copy(s_ref.at[e // 2], r_ref.at[q, e], own_sem)
+    own.start()
+    parts = [cp.start(s_ref.at[peer[1] // 2], r_ref.at[q, e], peer) for peer in far]
+    own.wait()
+    for part in parts:
+        part.wait_recv()
+    mine = r_ref.at[q]
+    a = cp.start(mine, mine, up)
+    b = cp.start(mine, mine, down)
+    co = [cp.start(mine, mine, core)]
+    a.wait_recv()
+    lo = r_ref.at[qd, pl.ds(0, 8)]
+    f = cp.start(lo, lo, up)
+    co.append(cp.start(r_ref.at[qd], r_ref.at[qd], core))
+    b.wait_recv()
+    hi = r_ref.at[qu, pl.ds(8, 8)]
+    g = cp.start(hi, hi, down)
+    co.append(cp.start(r_ref.at[qu], r_ref.at[qu], core))
+    f.wait_recv()
+    lo = r_ref.at[q2, pl.ds(0, 8)]
+    co.append(cp.start(lo, lo, core))
+    g.wait_recv()
+    hi = r_ref.at[q2, pl.ds(8, 8)]
+    co.append(cp.start(hi, hi, core))
+    for copy in co:
+        copy.wait_recv()
+    cp.finish()
+
+
+def slots_of(ids):
+    lane = lax.broadcasted_iota(jnp.int32, (TT, 128), 1)
+    row = lax.broadcasted_iota(jnp.int32, (TT, 128), 0)
+    hits = [(ids[:, k:k + 1] == lane).astype(F32) for k in range(2)]
+    lower = (lane < row).astype(F32).astype(BF16)
+    before = jnp.dot(lower, (hits[0] + hits[1]).astype(BF16), preferred_element_type=F32)
+    return [jnp.sum(hit * before, axis=1, keepdims=True).astype(jnp.int32) for hit in hits]
+
+
+def pack_kernel(ids_ref, x_ref, g_ref, s_ref):
+    ids = ids_ref[...]
+    slots = slots_of(ids)
+    lane = lax.broadcasted_iota(jnp.int32, (TT, 8 * CAP), 1)
+    hit = jnp.zeros((TT, 8 * CAP), F32)
+    for k in range(2):
+        hit = hit + (ids[:, k:k + 1] * CAP + slots[k] == lane).astype(F32)
+    hot = hit.T.astype(BF16)
+    for a, ref in enumerate((x_ref, g_ref)):
+        rows = jnp.dot(hot, ref[...], preferred_element_type=F32).astype(BF16)
+        for n in range(8):
+            s_ref[n, a] = rows[n * CAP:(n + 1) * CAP, :]
+
+
+def expert_kernel(r_ref, wg_ref, wu_ref, wd_ref, p_ref, pr_ref, gate, up, hid, dg, du):
+    i = pl.program_id(0)
+    nt = (((1,), (1,)), ((), ()))
+
+    @pl.when(i < 4)
+    def _():
+        x = jnp.concatenate([r_ref[:, n, 0].reshape(384, 256) for n in range(4)], axis=1)
+        g = jnp.concatenate([r_ref[:, n, 1].reshape(384, 256) for n in range(4)], axis=1)
+        a = jnp.dot(x, wg_ref[0], preferred_element_type=F32)
+        b = jnp.dot(x, wu_ref[0], preferred_element_type=F32)
+        d = lax.dot_general(g, wd_ref[0], nt, preferred_element_type=F32)
+
+        @pl.when(i == 0)
+        def _():
+            gate[...] = a
+            up[...] = b
+            hid[...] = d
+
+        @pl.when(i > 0)
+        def _():
+            gate[...] += a
+            up[...] += b
+            hid[...] += d
+
+    @pl.when(i == 3)
+    def _():
+        v, u, h = gate[...], up[...], hid[...]
+        sig = sigmoid(v)
+        act = v * sig
+        dg[...] = (h * u * sig * (1.0 + v * (1.0 - sig))).astype(BF16)
+        gu = h * act
+        du[...] = gu.astype(BF16)
+        pr_ref[...] = lax.dot_general(jnp.ones((8, 512), F32), gu * u, nt, preferred_element_type=F32,
+                                      precision=lax.Precision.HIGHEST)
+
+    @pl.when(i >= 4)
+    def _():
+        rows = lax.dot_general(dg[...], wg_ref[0], nt, preferred_element_type=F32)
+        rows = rows + lax.dot_general(du[...], wu_ref[0], nt, preferred_element_type=F32)
+        for n in range(4):
+            p_ref[:, n] = rows[:, n * 256:(n + 1) * 256].reshape(8, CAP, 256).astype(BF16)
+
+
+def added(out, first, *others):
+    total = first.astype(F32)
+    for other in others:
+        total = total + other.astype(F32)
+    return total.astype(out)
+
+
+class Ring:
+    def __init__(self, cp, place, up, down, block, land):
+        self.cp, self.p, self.up, self.down, self.block, self.land = cp, place, up, down, block, land
+
+    def at(self, step, half):
+        return self.block(lax.rem(self.p + step + 4, 4), half)
+
+    def first(self):
+        cp, land = self.cp, self.land
+        self.u2 = cp.start(self.at(2, 0), land.at[0], self.up)
+        self.d2 = cp.start(self.at(2, 1), land.at[1], self.down)
+        self.uh = cp.start(self.at(1, 1), land.at[2], self.up)
+        self.dl = cp.start(self.at(-1, 0), land.at[3], self.down)
+
+    def second(self, add):
+        cp, land = self.cp, self.land
+        self.u2.wait_recv()
+        add(land.at[6], self.at(1, 0), land.at[0])
+        self.ul = cp.start(land.at[6], land.at[4], self.up)
+        self.d2.wait_recv()
+        add(land.at[7], self.at(-1, 1), land.at[1])
+        self.dh = cp.start(land.at[7], land.at[5], self.down)
+
+    def last(self, add, outs):
+        land = self.land
+        self.dl.wait_recv()
+        self.ul.wait_recv()
+        add(outs[0], self.at(0, 0), land.at[4], land.at[3])
+        self.uh.wait_recv()
+        self.dh.wait_recv()
+        add(outs[1], self.at(0, 1), land.at[2], land.at[5])
+
+
+def add_rows(count):
+    def add(out, *refs):
+        @pl.loop(0, count)
+        def _(n):
+            out[n] = added(out.dtype, *[ref[n] for ref in refs])
+    return add
+
+
+def combine_kernel(p_ref, pr_ref, t_ref, tp_ref, pair, sums, land, final, probes, mine, send, recv, own_sem):
+    q, e = places()
+    y, c = q // 2, lax.rem(q, 2)
+    far = [(q, lax.rem(e + k, 16)) for k in range(1, 16)]
+    rows = [(lax.rem(q + k, 8), e) for k in range(1, 8)]
+    greet(far + rows)
+    up, down, core = (seq_at(y + 1, c), e), (seq_at(y - 1, c), e), (y * 2 + 1 - c, e)
+    cp = Copies(send, recv)
+    order = [2, 1, 3, 0]
+    halves = []
+    for n in order:
+        other = lax.rem(y + n, 4)
+        halves.append(cp.start(p_ref.at[other * 2 + 1 - c], pair.at[other], core))
+    tells = [cp.start(pr_ref, probes.at[k], rows[k]) for k in range(7)]
+    add = add_rows(8)
+
+    def block(d, half):
+        return sums.at[d, pl.ds(8 * half, 8)]
+
+    for n, copy in zip(order, halves):
+        other = lax.rem(y + n, 4)
+        copy.wait_recv()
+        add_rows(16)(sums.at[other], p_ref.at[other * 2 + c], pair.at[other])
+    ring = Ring(cp, y, up, down, block, land)
+    ring.first()
+    for tell in tells:
+        tell.wait_recv()
+    total = pr_ref[...]
+    for k in range(7):
+        total = total + probes[k]
+    mine[...] = pltpu.roll(total, lax.rem(8 - q, 8) * CAP, 1)[:, :128]
+    ring.second(add)
+    own_probe = pltpu.make_async_copy(mine, tp_ref.at[e], own_sem.at[0])
+    own_probe.start()
+    shares = [cp.start(mine, tp_ref.at[e], peer) for peer in far]
+    ring.last(add, (final.at[pl.ds(0, 8)], final.at[pl.ds(8, 8)]))
+    own = pltpu.make_async_copy(final.at[e], t_ref.at[e], own_sem.at[1])
+    own.start()
+    shares += [cp.start(final.at[peer[1]], t_ref.at[e], peer) for peer in far]
+    own_probe.wait()
+    own.wait()
+    for share in shares:
+        share.wait_recv()
+    cp.finish()
+
+
+def resid_kernel(ids_ref, w_ref, t_ref, tp_ref, g_ref, ow_ref, res_ref, probs_ref, i_ref, held):
+    @pl.when(pl.program_id(0) == 0)
+    def _():
+        ids = ids_ref[...]
+        slots = slots_of(ids)
+        lane = lax.broadcasted_iota(jnp.int32, (TT, 8 * CAP), 1)
+        near = lax.broadcasted_iota(jnp.int32, (TT, 128), 1)
+        total = g_ref[...].astype(F32)
+        even = jnp.concatenate([t_ref[2 * n] for n in range(8)], axis=0)
+        odd = jnp.concatenate([t_ref[2 * n + 1] for n in range(8)], axis=0)
+        probs = []
+        for k in range(2):
+            hot = (ids[:, k:k + 1] * CAP + slots[k] == lane).astype(F32).astype(BF16)
+            route = jnp.dot(hot, even, preferred_element_type=F32) + jnp.dot(hot, odd, preferred_element_type=F32)
+            total = total + w_ref[:, k:k + 1] * route
+            acc = jnp.zeros((TT, 128), F32)
+            for n in range(8):
+                row = tp_ref[2 * n, 0:1, :] + tp_ref[2 * n + 1, 0:1, :]
+                hit = (ids[:, k:k + 1] == n) & (slots[k] == near)
+                acc = acc + jnp.where(hit, row, 0.0)
+            probs.append(jnp.sum(acc, axis=1, keepdims=True))
+        held[...] = total.astype(BF16)
+        res_ref[...] = held[...]
+        probs_ref[...] = jnp.concatenate(probs, axis=1)
+
+    nt = (((1,), (1,)), ((), ()))
+    part = lax.dot_general(held[...], ow_ref[...], nt, preferred_element_type=F32)
+    for n in range(4):
+        i_ref[0, n] = part[:, n * 512:(n + 1) * 512].astype(BF16)
+
+
+def spread_kernel(i_ref, in_ref, lx, lz, kx, kz, jx, jz, send, recv):
+    q, e = places()
+    x, z = e // 4, lax.rem(e, 4)
+    xu, xd = (q, lax.rem(x + 1, 4) * 4 + z), (q, lax.rem(x + 3, 4) * 4 + z)
+    zu, zd = (q, x * 4 + lax.rem(z + 1, 4)), (q, x * 4 + lax.rem(z + 3, 4))
+    greet([xu, xd, zu, zd])
+    cp = Copies(send, recv)
+    rx = Ring(cp, x, xu, xd, lambda d, half: i_ref.at[d, pl.ds(2 * half, 2), pl.ds(0, 64)], lx)
+    rz = Ring(cp, z, zu, zd, lambda d, half: i_ref.at[pl.ds(2 * half, 2), d, pl.ds(64, 64)], lz)
+    two = add_rows(2)
+    rx.first()
+    rz.first()
+    rx.second(two)
+    rz.second(two)
+    rx.last(two, (jx.at[pl.ds(0, 2)], jx.at[pl.ds(2, 2)]))
+    sx = Ring(cp, z, zu, zd, lambda d, half: jx.at[d, pl.ds(32 * half, 32)], kx)
+    sx.first()
+    rz.last(two, (jz.at[pl.ds(0, 2)], jz.at[pl.ds(2, 2)]))
+    sz = Ring(cp, x, xu, xd, lambda d, half: jz.at[d, pl.ds(32 * half, 32)], kz)
+    sz.first()
+
+    def one(out, *refs):
+        out[...] = added(out.dtype, *[ref[...] for ref in refs])
+
+    sx.second(one)
+    sz.second(one)
+    sx.last(one, (in_ref.at[pl.ds(0, 32)], in_ref.at[pl.ds(32, 32)]))
+    sz.last(one, (in_ref.at[pl.ds(64, 32)], in_ref.at[pl.ds(96, 32)]))
+    cp.finish()
+
+
+def gather_kernel(pair_ref, all_ref, send, recv, own_sem):
+    q, e = places()
+    rows = [(lax.rem(q + k, 8), e) for k in range(1, 8)]
+    greet(rows)
+    cp = Copies(send, recv)
+    own = pltpu.make_async_copy(pair_ref, all_ref.at[q], own_sem)
+    own.start()
+    parts = [cp.start(pair_ref, all_ref.at[q], peer) for peer in rows]
+    own.wait()
+    for part in parts:
+        part.wait_recv()
+    cp.finish()
+
+
+def total_kernel(part_ref, out_ref, land, send, recv):
+    q, e = places()
+    rows = [(lax.rem(q + k, 8), e) for k in range(1, 8)]
+    greet(rows)
+    cp = Copies(send, recv)
+    parts = [cp.start(part_ref, land.at[q], peer) for peer in rows]
+    land[q] = part_ref[...]
+    for part in parts:
+        part.wait_recv()
+    total = land[0]
+    for k in range(1, 8):
+        total = total + land[k]
+    out_ref[...] = total
+    cp.finish()
+
+
+def sems(count):
+    return [pltpu.SemaphoreType.DMA((count,))] * 2
+
+
+def talk(number, limit=None):
+    return pltpu.CompilerParams(collective_id=number, has_side_effects=True, vmem_limit_bytes=limit)
 
 
 def local(
@@ -189,17 +505,90 @@
     skip_gain,
     block_states,
 ):
-    seq_count = lax.axis_size("seq")
-    exp_count = lax.axis_size("exp")
-    row_count, feat_cols = moe_input.shape
-    top_count = expert_ids.shape[1]
-    experts = exp_count // 2
-    capacity = 3 * top_count * row_count // (2 * experts)
     b_rep = jnp.repeat(state_input, GR, axis=0)
     c_rep = jnp.repeat(state_output, GR, axis=0)
     rates = log_rates.reshape(64, 128)
     start = block_states.reshape(64, 128)
     skip = jnp.tile(skip_gain.reshape(GR, 128), (2, 1))
+    packed = pl.pallas_call(
+        pack_kernel,
+        out_shape=shape((8, 2, CAP, 256), BF16),
+        in_specs=[VMEM] * 3,
+        out_specs=VMEM,
+        name="pack_rows",
+    )(expert_ids, moe_input, out_grad)
+    rows = pl.pallas_call(
+        dispatch_kernel,
+        out_shape=shape((8, 16, 2, CAP, 256), BF16),
+        in_specs=[ANY],
+        out_specs=ANY,
+        scratch_shapes=sems(24) + [pltpu.SemaphoreType.DMA],
+        compiler_params=talk(1),
+        name="dispatch",
+    )(packed)
+    parts, probes = pl.pallas_call(
+        expert_kernel,
+        grid=(8,),
+        out_shape=(shape((8, 16, CAP, 256), BF16), shape((8, 384))),
+        in_specs=[
+            pl.BlockSpec((8, 4, 2, CAP, 256), lambda i: (0, jnp.minimum(i, 3), 0, 0, 0)),
+            pl.BlockSpec((1, 1024, 512), lambda i: (0, lax.rem(i, 4), 0)),
+            pl.BlockSpec((1, 1024, 512), lambda i: (0, lax.rem(i, 4), 0)),
+            pl.BlockSpec((1, 512, 1024), lambda i: (0, 0, jnp.minimum(i, 3))),
+        ],
+        out_specs=(
+            pl.BlockSpec((8, 4, CAP, 256), lambda i: (0, jnp.maximum(i - 4, 0), 0, 0)),
+            pl.BlockSpec((8, 384), lambda i: (0, 0)),
+        ),
+        scratch_shapes=[pltpu.VMEM((384, 512), F32)] * 3 + [pltpu.VMEM((384, 512), BF16)] * 2,
+        name="experts",
+    )(rows, gate_weight, up_weight, down_weight)
+    returned, told = pl.pallas_call(
+        combine_kernel,
+        out_shape=(shape((16, CAP, 256), BF16), shape((16, 8, 128))),
+        in_specs=[VMEM] * 2,
+        out_specs=(VMEM,) * 2,
+        scratch_shapes=[
+            pltpu.VMEM((4, 16, CAP, 256), BF16),
+            pltpu.VMEM((4, 16, CAP, 256), BF16),
+            pltpu.VMEM((8, 8, CAP, 256), BF16),
+            pltpu.VMEM((16, CAP, 256), BF16),
+            pltpu.VMEM((7, 8, 384), F32),
+            pltpu.VMEM((8, 128), F32),
+        ] + sems(47) + [pltpu.SemaphoreType.DMA((2,))],
+        compiler_params=talk(2),
+        name="combine",
+    )(parts, probes)
+    resid_grad, probs_grad, inner_parts = pl.pallas_call(
+        resid_kernel,
+        grid=(4,),
+        out_shape=(shape((TT, 256), BF16), shape((TT, 2)), shape((4, 4, TT, 512), BF16)),
+        in_specs=[
+            pl.BlockSpec((TT, 2), lambda i: (0, 0)),
+            pl.BlockSpec((TT, 2), lambda i: (0, 0)),
+            pl.BlockSpec((16, CAP, 256), lambda i: (0, 0, 0)),
+            pl.BlockSpec((16, 8, 128), lambda i: (0, 0, 0)),
+            pl.BlockSpec((TT, 256), lambda i: (0, 0)),
+            pl.BlockSpec((2048, 256), lambda i: (i, 0)),
+        ],
+        out_specs=(
+            pl.BlockSpec((TT, 256), lambda i: (0, 0)),
+            pl.BlockSpec((TT, 2), lambda i: (0, 0)),
+            pl.BlockSpec((1, 4, TT, 512), lambda i: (i, 0, 0, 0)),
+        ),
+        scratch_shapes=[pltpu.VMEM((TT, 256), BF16)],
+        name="resid_and_inner",
+    )(expert_ids, expert_route_weights, returned, told, out_grad, out_weight)
+    inner_grad = pl.pallas_call(
+        spread_kernel,
+        out_shape=shape((TT, 512)),
+        in_specs=[VMEM],
+        out_specs=VMEM,
+        scratch_shapes=[pltpu.VMEM((8, 2, 64, 512), BF16)] * 2 + [pltpu.VMEM((8, 32, 512), F32)] * 2
+        + [pltpu.VMEM((4, 64, 512), F32)] * 2 + sems(24),
+        compiler_params=talk(3),
+        name="inner_sum",
+    )(inner_parts)
     earlier, steps, signal, scan_out = pl.pallas_call(
         forward_kernel,
         out_shape=(shape((TT * 64, 128)), shape((TT * 8, 128)), shape((TT * 8, 128)), shape((TT * 8, 128))),
@@ -207,54 +596,6 @@
         out_specs=(VMEM,) * 4,
         name="scan_forward",
     )(scan_input, delta_raw, b_rep, c_rep, rates, start, skip)
-    flat_ids = expert_ids.reshape(row_count * top_count)
-    matches = (flat_ids[:, None] == jnp.arange(experts, dtype=jnp.int32)[None, :]).astype(jnp.int32)
-    slot_ids = jnp.sum((jnp.cumsum(matches, axis=0) - matches) * matches, axis=1)
-    owners = jnp.arange(row_count * top_count, dtype=jnp.int32) // top_count
-    slot_table = jnp.zeros((capacity, experts), jnp.int32).at[slot_ids, flat_ids].set(owners)
-    send_in = moe_input[slot_table]
-    send_grad = out_grad[slot_table]
-
-    def widen_all(block):
-        wide = jnp.broadcast_to(
-            block[:, None, :, None, :], (capacity, seq_count, experts, 2, feat_cols)
-        )
-        return wide.reshape(capacity, seq_count * exp_count, feat_cols)
-
-    got_in, got_grad = (
-        lax.all_to_all(widen_all(send_in), ("seq", "exp"), split_axis=1, concat_axis=1, tiled=True),
-        lax.all_to_all(
-            widen_all(send_grad), ("seq", "exp"), split_axis=1, concat_axis=1, tiled=True
-        ),
-    )
-    rows_in = got_in.reshape(capacity * seq_count, exp_count * feat_cols)
-    rows_grad = got_grad.reshape(capacity * seq_count, exp_count * feat_cols)
-    partial_rows, probes = expert_backward(
-        rows_in, rows_grad, gate_weight[0], up_weight[0], down_weight[0]
-    )
-    part_back = partial_rows.reshape(capacity, seq_count * exp_count, feat_cols)
-    probe_back = jnp.broadcast_to(
-        probes.reshape(capacity, seq_count, 1, 1), (capacity, seq_count, exp_count, 1)
-    ).reshape(capacity, seq_count * exp_count, 1)
-    back_part, back_probe = (
-        lax.all_to_all(part_back, ("seq", "exp"), split_axis=1, concat_axis=1, tiled=True),
-        lax.all_to_all(probe_back, ("seq", "exp"), split_axis=1, concat_axis=1, tiled=True),
-    )
-    route_sum = jnp.sum(back_part.reshape(capacity, seq_count, experts, 2, feat_cols), axis=(1, 3))
-    probe_sum = jnp.sum(back_probe.reshape(capacity, seq_count, experts, 2), axis=(1, 3))
-    route_grad = route_sum[slot_ids, flat_ids].reshape(row_count, top_count, feat_cols)
-    probs_grad = probe_sum[slot_ids, flat_ids].reshape(row_count, top_count)
-    mixture = jnp.sum(expert_route_weights[:, :, None] * route_grad, axis=1)
-    resid_grad = (out_grad.astype(jnp.float32) + mixture).astype(jnp.bfloat16)
-    block = out_weight
-    inner_grad = lax.psum_scatter(
-        lax.dot_general(
-            block, resid_grad, (((1,), (1,)), ((), ())), preferred_element_type=jnp.float32
-        ),
-        "exp",
-        scatter_dimension=0,
-        tiled=True,
-    )
     y_grad, gate_grad, pair = pl.pallas_call(
         middle_kernel,
         out_shape=(shape((TT * 8, 128)), shape((512, 128), BF16), shape((128, 128))),
@@ -262,7 +603,15 @@
         out_specs=(VMEM,) * 3,
         name="adjoint_summary",
     )(inner_grad, mixer_gate_branch, c_rep, rates, steps, scan_out)
-    pairs = lax.all_gather(pair, "seq")
+    pairs = pl.pallas_call(
+        gather_kernel,
+        out_shape=shape((8, 128, 128)),
+        in_specs=[VMEM],
+        out_specs=VMEM,
+        scratch_shapes=sems(7) + [pltpu.SemaphoreType.DMA],
+        compiler_params=talk(4),
+        name="carry_gather",
+    )(pair)
     me = lax.axis_index("seq").astype(jnp.int32).reshape(1)
     input_grad, delta_grad, part = pl.pallas_call(
         final_kernel,
@@ -272,7 +621,15 @@
         scratch_shapes=[pltpu.VMEM((TT * 8, 128), F32)] * 2,
         name="adjoint_final",
     )(me, pairs, y_grad, earlier, steps, signal, delta_raw, b_rep, c_rep, rates, skip)
-    total = lax.psum(part, "seq")
+    total = pl.pallas_call(
+        total_kernel,
+        out_shape=shape((72, 128)),
+        in_specs=[VMEM],
+        out_specs=VMEM,
+        scratch_shapes=[pltpu.VMEM((8, 72, 128), F32)] + sems(7),
+        compiler_params=talk(5),
+        name="token_sums",
+    )(part)
     rates_grad = total[:64].reshape(16, 512)
     skip_grad = total[64:68].reshape(512)
     return (resid_grad, probs_grad, input_grad, delta_grad, gate_grad, rates_grad, skip_grad)

time: 399 us -> 197 us (0.49)
  waiting for transfers between devices: 190 us -> 0 us
  Pallas kernels: 31.8 us -> 187 us
  local copies, waits for them, and re-layouts: 61.5 us -> 8.54 us
  blocking collectives: 40.4 us -> 0 us
  starting transfers between devices: 27.9 us -> 0 us
  matrix products: 25.3 us -> 0 us
  between operations: 14.4 us -> 0.75 us
  other arithmetic: 4.46 us -> 0 us
    pallas_call x0 -> x8, Pallas kernels: none -> 155 us  [the longest x1 47.5 us: local(): pl.pallas_call(dispatch_kernel, out_shape=shape((8, 16, 2, CAP, 256), BF1...]
    all_to_all x4 -> x0, waiting for transfers between devices: 139 us -> none  [the longest x1 75.5 us: local(): lax.all_to_all(part_back, ('seq', 'exp'), split_axis=1, concat_axis=1, ti...]
    reduce_scatter x1 -> x0, waiting for transfers between devices: 51.4 us -> none  [local(): lax.psum_scatter(lax.dot_general(block, resid_grad, (((1,), (1,)), ((), (...]
    all_to_all x4 -> x0, starting transfers between devices: 27.9 us -> none  [the longest x1 11.5 us: local(): lax.all_to_all(widen_all(send_in), ('seq', 'exp'), split_axis=1, concat_a...]
    dot_general x6 -> x0, matrix products: 25.3 us -> none  [the longest x1 5.63 us: expert_backward(): lax.dot_general(rows_grad, down_slice, contract, preferred_element_type=j...]
    reshape x7 -> x0, local copies, waits for them, and re-layouts: 24.2 us -> none  [the longest x2 16.2 us: local(): part_back = partial_rows.reshape(capacity, seq_count * exp_count, feat_cols)]
    psum x1 -> x0, blocking collectives: 23.4 us -> none  [local(): total = lax.psum(part, 'seq')]
    all_gather x1 -> x0, blocking collectives: 17 us -> none  [local(): pairs = lax.all_gather(pair, 'seq')]
  transfers between devices with their start and end apart: 5 -> 0, of which waited for: 4 -> 0; matrix products, arithmetic and copies ran while one was open for 6% -> 0% of each run, Pallas kernels for 3% -> 0%
where the time goes in v1:
time: 197 us; the launch traced here: 196 us
  Pallas kernels  187 us (95%)
  local copies, waits for them, and re-layouts  8.54 us (4%)
    pallas_call x1, Pallas kernels, local(): pl.pallas_call(dispatch_kernel, out_shape=shape((8, 16, 2, CAP, 256), BF1...  47.5 us
    pallas_call x1, Pallas kernels, local(): pl.pallas_call(combine_kernel, out_shape=(shape((16, CAP, 256), BF16), sh...  36.2 us
    pallas_call x1, Pallas kernels, local(): pl.pallas_call(spread_kernel, out_shape=shape((TT, 512)), in_specs=[VMEM]...  23.1 us
    pallas_call x1, Pallas kernels, local(): pl.pallas_call(expert_kernel, grid=(8,), out_shape=(shape((8, 16, CAP, 25...  17 us
    pallas_call x1, Pallas kernels, local(): pl.pallas_call(gather_kernel, out_shape=shape((8, 128, 128)), in_specs=[V...  14.2 us
    pallas_call x1, Pallas kernels, local(): pl.pallas_call(final_kernel, out_shape=(shape((512, 128), BF16), shape((5...  11.7 us
    pallas_call x1, Pallas kernels, local(): pl.pallas_call(forward_kernel, out_shape=(shape((TT * 64, 128)), shape((T...  11.6 us
    pallas_call x1, Pallas kernels, local(): pl.pallas_call(total_kernel, out_shape=shape((72, 128)), in_specs=[VMEM],...  8.61 us

profile of v1, /device:TPU:1, one launch (start us, length us, event | category | flops | bytes accessed | tf_op | source)
XLA Modules:
  0.0 196.2 jit_solution(11552996114379156979)
XLA Ops:
  0.6 1.4 copy.24.ids_ref
  2.0 2.4 %pack_rows.1.s_ref = bf16[8,2,48,256]{3,2,1,0:T(8,128)(2,1)} custom-call(s32[128,2]{1,0:T(8,128)} %copy.24.ids_ref, bf16[128,256]{1,0:T(8,128)(2,1)} %x_ref.1, bf16[128,256]{1,0:T(8,128)(2,1)} %g_ref.3), custom_call_target="tpu_custom_call" | custom-call | tf_op jit(solution)/shard_map/pack_rows/pallas_call | solution.py:513
  4.4 47.5 %dispatch.1.r_ref = bf16[8,16,2,48,256]{4,3,2,1,0:T(8,128)(2,1)} custom-call(bf16[8,2,48,256]{3,2,1,0:T(8,128)(2,1)} %pack_rows.1.s_ref), custom_call_target="tpu_custom_call" | custom-call | tf_op jit(solution)/shard_map/dispatch/pallas_call | solution.py:520
  52.0 17.0 %experts.1 = (bf16[8,16,48,256]{3,2,1,0:T(8,128)(2,1)}, f32[8,384]{1,0:T(8,128)}) custom-call(bf16[8,16,2,48,256]{4,3,2,1,0:T(8,128)(2,1)} %dispatch.1.r_ref, bf16[1,4096,512]{2,1,0:T(8,128)(2,1)} %wg_ref.1, bf16[1,4096,512]{2,1,0:T(8,128)(2,1)} %wu_ref.1, bf16[1,512,4096]{2,1,0:T(8,128)(2,1)} %wd_ref.1), custom_call_target="tpu_custom_call" | custom-call | tf_op jit(solution)/shard_map/experts/pallas_call | solution.py:529
  69.0 36.2 %combine.1 = (bf16[16,48,256]{2,1,0:T(8,128)(2,1)}, f32[16,8,128]{2,1,0:T(8,128)}) custom-call(bf16[8,16,48,256]{3,2,1,0:T(8,128)(2,1)} %get-tuple-element.24.p_ref, f32[8,384]{1,0:T(8,128)} %get-tuple-element.25.pr_ref), custom_call_target="tpu_custom_call" | custom-call | tf_op jit(solution)/shard_map/combine/pallas_call | solution.py:546
  105.2 0.0 copy-start.3
  105.3 0.0 copy-start.1
  105.3 0.7 copy.25.w_ref
  106.1 6.0 %resid_and_inner.1 = (bf16[128,256]{1,0:T(8,128)(2,1)}, f32[128,2]{1,0:T(8,128)}, bf16[4,4,128,512]{3,2,1,0:T(8,128)(2,1)}) custom-call(s32[128,2]{1,0:T(8,128)} %copy.24.ids_ref, f32[128,2]{1,0:T(8,128)} %copy.25.w_ref, bf16[16,48,256]{2,1,0:T(8,128)(2,1)} %get-tuple-element.26.t_ref, f32[16,8,128]{2,1,0:T(8,128)} %get-tuple-element.27.tp_ref, ...), custom_call_target="tpu_custom_call" | custom-call | tf_op jit(solution)/shard_map/resid_and_inner/pallas_call | solution.py:562
  112.1 23.1 %inner_sum.1.in_ref = f32[128,512]{1,0:T(8,128)} custom-call(bf16[4,4,128,512]{3,2,1,0:T(8,128)(2,1)} %get-tuple-element.30.i_ref), custom_call_target="tpu_custom_call" | custom-call | tf_op jit(solution)/shard_map/inner_sum/pallas_call | solution.py:582
  135.2 0.6 broadcast_in_dim.6
  135.8 0.6 reshape.41.lr_ref
  136.4 0.6 broadcast_in_dim.7
  137.1 0.6 tile.11
  137.7 0.6 reshape.43.st_ref
  138.3 11.6 %scan_forward.1 = (f32[8192,128]{1,0:T(8,128)}, f32[1024,128]{1,0:T(8,128)}, f32[1024,128]{1,0:T(8,128)}, f32[1024,128]{1,0:T(8,128)}) custom-call(bf16[512,128]{1,0:T(8,128)(2,1)} %u_ref.1, bf16[512,128]{1,0:T(8,128)(2,1)} %d_ref.3, f32[64,128]{1,0:T(8,128)} %bitcast.10, f32[64,128]{1,0:T(8,128)} %bitcast.7, f32[64,128]{1,0:T(8,128)} %reshape.41.lr_ref, ...), custom_call_target="tpu_custom_call" | custom-call | tf_op jit(solution)/shard_map/scan_forward/pallas_call | solution.py:592
  149.9 8.5 %adjoint_summary.1 = (f32[1024,128]{1,0:T(8,128)}, bf16[512,128]{1,0:T(8,128)(2,1)}, f32[128,128]{1,0:T(8,128)}) custom-call(f32[128,512]{1,0:T(8,128)} %inner_sum.1.in_ref, bf16[512,128]{1,0:T(8,128)(2,1)} %z_ref.1, f32[64,128]{1,0:T(8,128)} %bitcast.8, f32[64,128]{1,0:T(8,128)} %reshape.41.lr_ref, f32[1024,128]{1,0:T(8,128)} %get-tuple-element.31.dt_ref, ...), custom_call_target="tpu_custom_call" | custom-call | tf_op jit(solution)/shard_map/adjoint_summary/pallas_call | solution.py:599
  158.3 14.2 %carry_gather.1.all_ref = f32[8,128,128]{2,1,0:T(8,128)} custom-call(f32[128,128]{1,0:T(8,128)} %get-tuple-element.33.pair_ref), custom_call_target="tpu_custom_call" | custom-call | tf_op jit(solution)/shard_map/carry_gather/pallas_call | solution.py:606
  172.6 11.7 %adjoint_final.1 = (bf16[512,128]{1,0:T(8,128)(2,1)}, bf16[512,128]{1,0:T(8,128)(2,1)}, f32[72,128]{1,0:T(8,128)}) custom-call(s32[1]{0:T(128)} %bitcast.me_ref, f32[8,128,128]{2,1,0:T(8,128)} %carry_gather.1.all_ref, f32[1024,128]{1,0:T(8,128)} %get-tuple-element.34.y_ref, f32[8192,128]{1,0:T(8,128)} %get-tuple-element.35.ear_ref, ...), custom_call_target="tpu_custom_call" | custom-call | tf_op jit(solution)/shard_map/adjoint_final/pallas_call | solution.py:616
  184.3 8.6 %token_sums.1 = f32[72,128]{1,0:T(8,128)} custom-call(f32[72,128]{1,0:T(8,128)} %get-tuple-element.40.part_ref), custom_call_target="tpu_custom_call" | custom-call | tf_op jit(solution)/shard_map/token_sums/pallas_call | solution.py:624
  192.9 0.8 slice.6
  193.7 0.6 reshape.44
  194.3 1.3 slice_bitcast_fusion
  195.6 0.6 copy.26
  (12 shorter events, 0.0 us)
Async XLA Ops:
  52.0 53.3 %copy-start.6 = (f32[128,2]{0,1:T(2,128)S(1)}, f32[128,2]{0,1:T(2,128)}, u32[]{:S(2)}) copy-start(f32[128,2]{0,1:T(2,128)} %param.19) | copy-start | bytes 3076
  105.2 30.0 %copy-start.3 = (f32[16,128]{1,0:T(8,128)S(1)}, f32[16,128]{1,0:T(8,128)}, u32[]{:S(2)}) copy-start(f32[16,128]{1,0:T(8,128)} %param.28) | copy-start | bytes 24580
  105.3 30.6 %copy-start.1 = (f32[16,512]{1,0:T(8,128)S(1)}, f32[16,512]{1,0:T(8,128)}, u32[]{:S(2)}) copy-start(f32[16,512]{1,0:T(8,128)} %param.29) | copy-start | bytes 98308
  105.3 31.2 %copy-start.4 = (f32[16,128]{1,0:T(8,128)S(1)}, f32[16,128]{1,0:T(8,128)}, u32[]{:S(2)}) copy-start(f32[16,128]{1,0:T(8,128)} %param.27) | copy-start | bytes 24580
  105.3 31.8 %copy-start.5 = (f32[512]{0:T(512)S(1)}, f32[512]{0:T(512)}, u32[]{:S(2)}) copy-start(f32[512]{0:T(512)} %param.30) | copy-start | bytes 6148
  105.3 32.4 %copy-start.2 = (f32[1,16,512]{2,1,0:T(8,128)S(1)}, f32[1,16,512]{2,1,0:T(8,128)}, u32[]{:S(2)}) copy-start(f32[1,16,512]{2,1,0:T(8,128)} %param.31) | copy-start | bytes 98308
  149.9 45.7 %copy-start = (f32[128,2]{1,0:T(8,128)S(1)}, f32[128,2]{1,0:T(8,128)}, u32[]{:S(2)}) copy-start(f32[128,2]{1,0:T(8,128)} %get-tuple-element.42) | copy-start | bytes 3076

commit v2 on v1

--- a/solution.py
+++ b/solution.py
@@ -19,6 +19,7 @@
 LOG2E = 1.4426950408889634
 GR = 4
 TT = 128
+ROWS = 64
 
 
 def softplus(v):
@@ -38,114 +39,78 @@
     return jnp.take_along_axis(rep, jnp.full((8, 128), t, jnp.int32), axis=1)
 
 
-def forward_kernel(u_ref, d_ref, b_ref, c_ref, lr_ref, st_ref, sk_ref, ear_ref, dt_ref, us_ref, so_ref):
-    for g in range(GR):
-        rows = pl.ds(g * 128, 128)
-        spread(dt_ref, g, softplus(d_ref[rows, :].astype(jnp.float32).T))
-        spread(us_ref, g, u_ref[rows, :].astype(jnp.float32).T)
-    rate2 = [-LOG2E * jnp.exp(lr_ref[8 * j:8 * j + 8, :]) for j in range(8)]
-    skip = sk_ref[...]
-
-    def step(t, states):
-        here = pl.ds(pl.multiple_of(t * 8, 8), 8)
-        dt = dt_ref[here, :]
-        u = us_ref[here, :]
-        du = dt * u
-        acc = jnp.zeros((8, 128), jnp.float32)
-        out = []
+def grouped(ref, j):
+    return jnp.concatenate(
+        [ref[2 * j + p:2 * j + p + 1, g * 128:(g + 1) * 128] for p in range(2) for g in range(GR)], axis=0)
+
+
+def doubled(ref, j):
+    return jnp.concatenate(
+        [jnp.broadcast_to(ref[2 * j + p:2 * j + p + 1, :], (GR, 128)) for p in range(2)], axis=0)
+
+
+def octet(j):
+    return slice(8 * j, 8 * j + 8)
+
+
+def at_token(t):
+    return pl.ds(pl.multiple_of(t * 8, 8), 8)
+
+
+def at_state(t, j):
+    return pl.ds(pl.multiple_of(t * ROWS, ROWS) + 8 * j, 8)
+
+
+class Forward:
+    def __init__(self, u, d, b, c, lr, st, sk, rate, decay, skip, a, ear, bb, cb, dt, us, so):
+        self.__dict__.update(locals())
+
+    def open(self):
+        for g in range(GR):
+            rows = pl.ds(g * 128, 128)
+            spread(self.dt, g, softplus(self.d[rows, :].astype(F32).T))
+            spread(self.us, g, self.u[rows, :].astype(F32).T)
         for j in range(8):
-            ear_ref[pl.ds(pl.multiple_of(t * 64, 64) + 8 * j, 8), :] = states[j]
-            b = column(b_ref[8 * j:8 * j + 8, :], t)
-            c = column(c_ref[8 * j:8 * j + 8, :], t)
-            state = jnp.exp2(dt * rate2[j]) * states[j] + du * b
-            acc = acc + c * state
-            out.append(state)
-        so_ref[here, :] = acc + pltpu.roll(acc, 4, 0) + skip * u
-        return tuple(out)
-
-    lax.fori_loop(0, TT, step, tuple(st_ref[8 * j:8 * j + 8, :] for j in range(8)), unroll=2)
-
-
-def middle_kernel(in_ref, z_ref, c_ref, lr_ref, dt_ref, so_ref, y_ref, gate_ref, pair_ref):
-    for g in range(GR):
-        rows = pl.ds(g * 128, 128)
-        up = in_ref[:, rows]
-        z = z_ref[rows, :].astype(jnp.float32).T
-        sig = sigmoid(z)
-        spread(y_ref, g, up * z * sig)
-        so = so_ref[pl.ds(g, TT, stride=8), :]
-        gate_ref[rows, :] = (up * so * sig * (1.0 + z * (1.0 - sig))).T.astype(jnp.bfloat16)
-    rate2 = [-LOG2E * jnp.exp(lr_ref[8 * j:8 * j + 8, :]) for j in range(8)]
-
-    def step(i, carry):
-        t = TT - 1 - i
-        here = pl.ds(pl.multiple_of(t * 8, 8), 8)
-        dt = dt_ref[here, :]
-        y = y_ref[here, :]
-        total = carry[8] + dt
-        out = []
+            self.rate[octet(j), :] = jnp.exp(grouped(self.lr, j))
+        self.skip[...] = jnp.concatenate(
+            [self.sk[0:1, g * 128:(g + 1) * 128] for p in range(2) for g in range(GR)], axis=0)
+        one = jnp.ones((8, 128), F32)
+        return tuple(grouped(self.st.at[0], j) for j in range(8)) + (one,) * 8
+
+    def run(self, first, last, carry):
+        rate2 = [-LOG2E * self.rate[octet(j), :] for j in range(8)]
+        b_rep = [doubled(self.b, j) for j in range(8)]
+        c_rep = [doubled(self.c, j) for j in range(8)]
+        skip = self.skip[...]
+
+        def step(t, carry):
+            here = at_token(t)
+            dt = self.dt[here, :]
+            u = self.us[here, :]
+            du = dt * u
+            acc = jnp.zeros((8, 128), F32)
+            states, products = [], []
+            for j in range(8):
+                spot = at_state(t, j)
+                b = column(b_rep[j], t)
+                c = column(c_rep[j], t)
+                a = jnp.exp2(dt * rate2[j])
+                state = a * carry[j] + du * b
+                self.ear[spot, :] = carry[j]
+                self.a[spot, :] = a
+                self.bb[spot, :] = b
+                self.cb[spot, :] = c
+                acc = acc + c * state
+                states.append(state)
+                products.append(carry[8 + j] * a)
+            self.so[here, :] = acc + pltpu.roll(acc, 4, 0) + skip * u
+            return tuple(states + products)
+
+        return lax.fori_loop(first, last, step, carry)
+
+    def close(self, carry):
         for j in range(8):
-            c = column(c_ref[8 * j:8 * j + 8, :], t)
-            out.append(jnp.exp2(dt * rate2[j]) * (c * y + carry[j]))
-        return tuple(out) + (total,)
-
-    zero = jnp.zeros((8, 128), jnp.float32)
-    last = lax.fori_loop(0, TT, step, (zero,) * 9, unroll=2)
-    for j in range(8):
-        pair_ref[8 * j:8 * j + 8, :] = last[j]
-        pair_ref[64 + 8 * j:72 + 8 * j, :] = jnp.exp2(rate2[j] * last[8])
-
-
-def final_kernel(me_ref, all_ref, y_ref, ear_ref, dt_ref, us_ref, d_ref, b_ref, c_ref, lr_ref, sk_ref,
-                 input_ref, delta_ref, part_ref, s1_ref, dl_ref):
-    me = me_ref[0]
-    rate = [jnp.exp(lr_ref[8 * j:8 * j + 8, :]) for j in range(8)]
-    rate2 = [-LOG2E * rate[j] for j in range(8)]
-    start = []
-    for j in range(8):
-        inc = jnp.zeros((8, 128), jnp.float32)
-        for r in range(N_SEQ - 1, 0, -1):
-            term = all_ref[r, 8 * j:8 * j + 8, :]
-            decay = all_ref[r, 64 + 8 * j:72 + 8 * j, :]
-            inc = jnp.where(r > me, term + decay * inc, inc)
-        start.append(inc)
-
-    def step(i, carry):
-        vs, sums, sk = carry
-        t = TT - 1 - i
-        here = pl.ds(pl.multiple_of(t * 8, 8), 8)
-        dt = dt_ref[here, :]
-        y = y_ref[here, :]
-        s1 = jnp.zeros((8, 128), jnp.float32)
-        dl = jnp.zeros((8, 128), jnp.float32)
-        nv, ns = [], []
-        for j in range(8):
-            b = column(b_ref[8 * j:8 * j + 8, :], t)
-            c = column(c_ref[8 * j:8 * j + 8, :], t)
-            adj = c * y + vs[j]
-            v = jnp.exp2(dt * rate2[j]) * adj
-            x = v * ear_ref[pl.ds(pl.multiple_of(t * 64, 64) + 8 * j, 8), :]
-            s1 = s1 + adj * b
-            dl = dl + rate[j] * x
-            ns.append(sums[j] + dt * x)
-            nv.append(v)
-        s1_ref[here, :] = s1 + pltpu.roll(s1, 4, 0)
-        dl_ref[here, :] = dl + pltpu.roll(dl, 4, 0)
-        return tuple(nv), tuple(ns), sk + y * us_ref[here, :]
-
-    zero = jnp.zeros((8, 128), jnp.float32)
-    vs, sums, sk = lax.fori_loop(0, TT, step, (tuple(start), (zero,) * 8, zero), unroll=2)
-    for j in range(8):
-        part_ref[8 * j:8 * j + 8, :] = -rate[j] * sums[j]
-    part_ref[64:72, :] = sk
-    for g in range(GR):
-        rows = pl.ds(g * 128, 128)
-        mine = pl.ds(g, TT, stride=8)
-        s1 = s1_ref[mine, :]
-        inp = s1 * dt_ref[mine, :] + sk_ref[g:g + 1, :] * y_ref[mine, :]
-        input_ref[rows, :] = inp.T.astype(jnp.bfloat16)
-        step_grad = us_ref[mine, :] * s1 - dl_ref[mine, :]
-        delta_ref[rows, :] = (step_grad.T * sigmoid(d_ref[rows, :].astype(jnp.float32))).astype(jnp.bfloat16)
+            self.decay[octet(j), :] = carry[8 + j]
 
 
 MESH = pl.DeviceIdType.MESH
@@ -170,13 +135,16 @@
     def __init__(self, send, recv):
         self.send, self.recv, self.all, self.next = send, recv, [], 0
 
-    def start(self, src, dst, peer):
+    def make(self, src, dst, peer):
         n = self.next
         self.next = n + 1
-        copy = pltpu.make_async_remote_copy(
+        return pltpu.make_async_remote_copy(
             src_ref=src, dst_ref=dst, send_sem=self.send.at[n], recv_sem=self.recv.at[n],
             device_id=peer, device_id_type=MESH,
         )
+
+    def start(self, src, dst, peer):
+        copy = self.make(src, dst, peer)
         copy.start()
         self.all.append(copy)
         return copy
@@ -190,7 +158,8 @@
     return lax.rem(y + 4, 4) * 2 + c
 
 
-def dispatch_kernel(s_ref, r_ref, send, recv, own_sem):
+def dispatch_kernel(s_ref, u, d, b_ref, c_ref, lr, st, sk, r_ref, a_h, ear_h, bb_h, cb_h, dt_h, us_h, so_h, rate, decay, skip,
+                    a_v, ear, bb, cb, dt, us, so, send, recv, own_sem, near):
     q, e = places()
     y, c = q // 2, lax.rem(q, 2)
     qu, qd, q2, qc = seq_at(y + 1, c), seq_at(y - 1, c), seq_at(y + 2, c), y * 2 + 1 - c
@@ -201,6 +170,8 @@
     own = pltpu.make_async_copy(s_ref.at[e // 2], r_ref.at[q, e], own_sem)
     own.start()
     parts = [cp.start(s_ref.at[peer[1] // 2], r_ref.at[q, e], peer) for peer in far]
+    scan = Forward(u, d, b_ref, c_ref, lr, st, sk, rate, decay, skip, a_v, ear, bb, cb, dt, us, so)
+    carry = scan.run(0, 64, scan.open())
     own.wait()
     for part in parts:
         part.wait_recv()
@@ -208,6 +179,11 @@
     a = cp.start(mine, mine, up)
     b = cp.start(mine, mine, down)
     co = [cp.start(mine, mine, core)]
+    scan.close(scan.run(64, TT, carry))
+    saves = [pltpu.make_async_copy(src, dst, near.at[n]) for n, (src, dst) in enumerate(
+        ((a_v, a_h), (ear, ear_h), (bb, bb_h), (cb, cb_h), (dt, dt_h), (us, us_h), (so, so_h)))]
+    for save in saves:
+        save.start()
     a.wait_recv()
     lo = r_ref.at[qd, pl.ds(0, 8)]
     f = cp.start(lo, lo, up)
@@ -224,6 +200,8 @@
     co.append(cp.start(hi, hi, core))
     for copy in co:
         copy.wait_recv()
+    for save in saves:
+        save.wait()
     cp.finish()
 
 
@@ -304,15 +282,15 @@
     def __init__(self, cp, place, up, down, block, land):
         self.cp, self.p, self.up, self.down, self.block, self.land = cp, place, up, down, block, land
 
-    def at(self, step, half):
-        return self.block(lax.rem(self.p + step + 4, 4), half)
+    def at(self, step, half, own=1):
+        return self.block(lax.rem(self.p + step + 4, 4), half)[own]
 
     def first(self):
         cp, land = self.cp, self.land
-        self.u2 = cp.start(self.at(2, 0), land.at[0], self.up)
-        self.d2 = cp.start(self.at(2, 1), land.at[1], self.down)
-        self.uh = cp.start(self.at(1, 1), land.at[2], self.up)
-        self.dl = cp.start(self.at(-1, 0), land.at[3], self.down)
+        self.u2 = cp.start(self.at(2, 0, 0), land.at[0], self.up)
+        self.d2 = cp.start(self.at(2, 1, 0), land.at[1], self.down)
+        self.uh = cp.start(self.at(1, 1, 0), land.at[2], self.up)
+        self.dl = cp.start(self.at(-1, 0, 0), land.at[3], self.down)
 
     def second(self, add):
         cp, land = self.cp, self.land
@@ -358,7 +336,7 @@
     add = add_rows(8)
 
     def block(d, half):
-        return sums.at[d, pl.ds(8 * half, 8)]
+        return (sums.at[d, pl.ds(8 * half, 8)],) * 2
 
     for n, copy in zip(order, halves):
         other = lax.rem(y + n, 4)
@@ -418,25 +396,71 @@
         i_ref[0, n] = part[:, n * 512:(n + 1) * 512].astype(BF16)
 
 
-def spread_kernel(i_ref, in_ref, lx, lz, kx, kz, jx, jz, send, recv):
+def sems(count):
+    return [pltpu.SemaphoreType.DMA((count,))] * 2
+
+
+def talk(number, limit=None):
+    return pltpu.CompilerParams(collective_id=number, has_side_effects=True, vmem_limit_bytes=limit)
+
+
+def tail_kernel(i_ref, a_h, ear_h, bb_h, cb_h, dt_h, us_h, so_h, z_ref, d_ref, rate_ref, decay_ref, skip_ref,
+                gate_ref, input_ref, delta_ref, rates_ref, skipped_ref,
+                ivm, lx, lz, kx, kz, jx, jz, inner, a, ear, bb, cb, dt, us, so, ys, s1s, dls,
+                term, terms, decays, part, other, both, three, send, recv, near):
     q, e = places()
     x, z = e // 4, lax.rem(e, 4)
+    y, c = q // 2, lax.rem(q, 2)
     xu, xd = (q, lax.rem(x + 1, 4) * 4 + z), (q, lax.rem(x + 3, 4) * 4 + z)
     zu, zd = (q, x * 4 + lax.rem(z + 1, 4)), (q, x * 4 + lax.rem(z + 3, 4))
-    greet([xu, xd, zu, zd])
+    loads = [pltpu.make_async_copy(src, dst, near.at[n]) for n, (src, dst) in enumerate(
+        ((i_ref, ivm), (dt_h, dt), (us_h, us), (so_h, so), (a_h, a), (cb_h, cb), (ear_h, ear), (bb_h, bb)))]
+    for load in loads:
+        load.start()
+    terms[...] = jnp.zeros_like(terms)
+    decays[...] = jnp.zeros_like(decays)
+    greet([xu, xd, zu, zd] + [(lax.rem(q + k, 8), e) for k in range(1, 8)])
     cp = Copies(send, recv)
-    rx = Ring(cp, x, xu, xd, lambda d, half: i_ref.at[d, pl.ds(2 * half, 2), pl.ds(0, 64)], lx)
-    rz = Ring(cp, z, zu, zd, lambda d, half: i_ref.at[pl.ds(2 * half, 2), d, pl.ds(64, 64)], lz)
+
+    def earlier_shards(src, land):
+        copies = []
+        for k in range(1, 8):
+            copy = cp.make(src, land.at[k - 1], (lax.rem(q + 8 - k, 8), e))
+
+            @pl.when(q >= k)
+            def _(copy=copy):
+                copy.start()
+            copies.append(copy)
+
+        def arrive():
+            for k in range(1, 8):
+                @pl.when(q + k < 8)
+                def _(k=k):
+                    copies[k - 1].wait_recv()
+
+        def leave():
+            for k in range(1, 8):
+                @pl.when(q >= k)
+                def _(k=k):
+                    copies[k - 1].wait_send()
+        return arrive, leave
+
+    rx = Ring(cp, x, xu, xd, lambda d, half: (i_ref.at[d, pl.ds(2 * half, 2), pl.ds(0, 64)],
+                                              ivm.at[d, pl.ds(2 * half, 2), pl.ds(0, 64)]), lx)
+    rz = Ring(cp, z, zu, zd, lambda d, half: (i_ref.at[pl.ds(2 * half, 2), d, pl.ds(64, 64)],
+                                              ivm.at[pl.ds(2 * half, 2), d, pl.ds(64, 64)]), lz)
     two = add_rows(2)
     rx.first()
     rz.first()
+    decays_in, decays_out = earlier_shards(decay_ref, decays)
+    loads[0].wait()
     rx.second(two)
     rz.second(two)
     rx.last(two, (jx.at[pl.ds(0, 2)], jx.at[pl.ds(2, 2)]))
-    sx = Ring(cp, z, zu, zd, lambda d, half: jx.at[d, pl.ds(32 * half, 32)], kx)
+    sx = Ring(cp, z, zu, zd, lambda d, half: (jx.at[d, pl.ds(32 * half, 32)],) * 2, kx)
     sx.first()
     rz.last(two, (jz.at[pl.ds(0, 2)], jz.at[pl.ds(2, 2)]))
-    sz = Ring(cp, x, xu, xd, lambda d, half: jz.at[d, pl.ds(32 * half, 32)], kz)
+    sz = Ring(cp, x, xu, xd, lambda d, half: (jz.at[d, pl.ds(32 * half, 32)],) * 2, kz)
     sz.first()
 
     def one(out, *refs):
@@ -444,47 +468,107 @@
 
     sx.second(one)
     sz.second(one)
-    sx.last(one, (in_ref.at[pl.ds(0, 32)], in_ref.at[pl.ds(32, 32)]))
-    sz.last(one, (in_ref.at[pl.ds(64, 32)], in_ref.at[pl.ds(96, 32)]))
+    sx.last(one, (inner.at[pl.ds(0, 32)], inner.at[pl.ds(32, 32)]))
+    sz.last(one, (inner.at[pl.ds(64, 32)], inner.at[pl.ds(96, 32)]))
+    for load in loads[1:]:
+        load.wait()
+
+    for g in range(GR):
+        rows = pl.ds(g * 128, 128)
+        act = z_ref[rows, :].astype(F32).T
+        spread(ys, g, inner[:, rows] * act * sigmoid(act))
+
+    zero = jnp.zeros((8, 128), F32)
+
+    def summary(i, carry):
+        t = TT - 1 - i
+        grad = ys[at_token(t), :]
+        return tuple(a[at_state(t, j), :] * (cb[at_state(t, j), :] * grad + carry[j]) for j in range(8))
+
+    last = lax.fori_loop(0, TT, summary, (zero,) * 8, unroll=4)
+    for j in range(8):
+        term[octet(j), :] = last[j]
+    terms_in, terms_out = earlier_shards(term, terms)
+
+    for g in range(GR):
+        rows = pl.ds(g * 128, 128)
+        act = z_ref[rows, :].astype(F32).T
+        sig = sigmoid(act)
+        gated = inner[:, rows] * so[pl.ds(g, TT, stride=8), :] * sig * (1.0 + act * (1.0 - sig))
+        gate_ref[rows, :] = gated.T.astype(BF16)
+
+    decays_in()
+    terms_in()
+    rate = [rate_ref[octet(j), :] for j in range(8)]
+    start = []
+    for j in range(8):
+        inc = zero
+        for k in range(7, 0, -1):
+            inc = terms[k - 1, octet(j), :] + decays[k - 1, octet(j), :] * inc
+        start.append(inc)
+
+    def step(i, carry):
+        vs, sums, sk = carry
+        t = TT - 1 - i
+        here = at_token(t)
+        grad = ys[here, :]
+        size = dt[here, :]
+        s1, dl = zero, zero
+        nv, ns = [], []
+        for j in range(8):
+            spot = at_state(t, j)
+            adj = cb[spot, :] * grad + vs[j]
+            v = a[spot, :] * adj
+            w = v * ear[spot, :]
+            s1 = s1 + adj * bb[spot, :]
+            dl = dl + rate[j] * w
+            ns.append(sums[j] + size * w)
+            nv.append(v)
+        s1s[here, :] = s1 + pltpu.roll(s1, 4, 0)
+        dls[here, :] = dl + pltpu.roll(dl, 4, 0)
+        return tuple(nv), tuple(ns), sk + grad * us[here, :]
+
+    vs, sums, sk = lax.fori_loop(0, TT, step, (tuple(start), (zero,) * 8, zero), unroll=2)
+    for j in range(8):
+        part[octet(j), :] = -rate[j] * sums[j]
+    part[64:72, :] = sk
+    swap = cp.start(part, other, (y * 2 + 1 - c, e))
+
+    for g in range(GR):
+        rows = pl.ds(g * 128, 128)
+        mine = pl.ds(g, TT, stride=8)
+        s1 = s1s[mine, :]
+        inp = s1 * dt[mine, :] + skip_ref[g:g + 1, :] * ys[mine, :]
+        input_ref[rows, :] = inp.T.astype(BF16)
+
+    swap.wait_recv()
+    both[...] = part[...] + other[...]
+    shares = [cp.start(both, three.at[k - 1], (seq_at(y + k, c), e)) for k in range(1, 4)]
+
+    for g in range(GR):
+        rows = pl.ds(g * 128, 128)
+        mine = pl.ds(g, TT, stride=8)
+        step_grad = us[mine, :] * s1s[mine, :] - dls[mine, :]
+        delta_ref[rows, :] = (step_grad.T * sigmoid(d_ref[rows, :].astype(F32))).astype(BF16)
+
+    for share in shares:
+        share.wait_recv()
+    both2 = both[...] + three[0] + three[1] + three[2]
+    for j in range(8):
+        for p in range(2):
+            for g in range(GR):
+                row = 8 * j + GR * p + g
+                rates_ref[2 * j + p:2 * j + p + 1, g * 128:(g + 1) * 128] = both2[row:row + 1, :]
+    for g in range(GR):
+        skipped_ref[0:1, g * 128:(g + 1) * 128] = both2[64 + g:65 + g, :]
+    decays_out()
+    terms_out()
     cp.finish()
 
 
-def gather_kernel(pair_ref, all_ref, send, recv, own_sem):
-    q, e = places()
-    rows = [(lax.rem(q + k, 8), e) for k in range(1, 8)]
-    greet(rows)
-    cp = Copies(send, recv)
-    own = pltpu.make_async_copy(pair_ref, all_ref.at[q], own_sem)
-    own.start()
-    parts = [cp.start(pair_ref, all_ref.at[q], peer) for peer in rows]
-    own.wait()
-    for part in parts:
-        part.wait_recv()
-    cp.finish()
-
-
-def total_kernel(part_ref, out_ref, land, send, recv):
-    q, e = places()
-    rows = [(lax.rem(q + k, 8), e) for k in range(1, 8)]
-    greet(rows)
-    cp = Copies(send, recv)
-    parts = [cp.start(part_ref, land.at[q], peer) for peer in rows]
-    land[q] = part_ref[...]
-    for part in parts:
-        part.wait_recv()
-    total = land[0]
-    for k in range(1, 8):
-        total = total + land[k]
-    out_ref[...] = total
-    cp.finish()
-
-
-def sems(count):
-    return [pltpu.SemaphoreType.DMA((count,))] * 2
-
-
-def talk(number, limit=None):
-    return pltpu.CompilerParams(collective_id=number, has_side_effects=True, vmem_limit_bytes=limit)
+def finish_kernel(*refs):
+    for src, dst in zip(refs[:5], refs[5:]):
+        dst[...] = src[...]
 
 
 def local(
@@ -505,11 +589,6 @@
     skip_gain,
     block_states,
 ):
-    b_rep = jnp.repeat(state_input, GR, axis=0)
-    c_rep = jnp.repeat(state_output, GR, axis=0)
-    rates = log_rates.reshape(64, 128)
-    start = block_states.reshape(64, 128)
-    skip = jnp.tile(skip_gain.reshape(GR, 128), (2, 1))
     packed = pl.pallas_call(
         pack_kernel,
         out_shape=shape((8, 2, CAP, 256), BF16),
@@ -517,15 +596,19 @@
         out_specs=VMEM,
         name="pack_rows",
     )(expert_ids, moe_input, out_grad)
-    rows = pl.pallas_call(
+    big = shape((TT * ROWS, 128))
+    wide = shape((TT * 8, 128))
+    rows, *saved, rate, decay, skip = pl.pallas_call(
         dispatch_kernel,
-        out_shape=shape((8, 16, 2, CAP, 256), BF16),
-        in_specs=[ANY],
-        out_specs=ANY,
-        scratch_shapes=sems(24) + [pltpu.SemaphoreType.DMA],
+        out_shape=(shape((8, 16, 2, CAP, 256), BF16), big, big, big, big, wide, wide, wide,
+                   shape((ROWS, 128)), shape((ROWS, 128)), shape((8, 128))),
+        in_specs=[ANY] + [VMEM] * 7,
+        out_specs=(ANY,) * 8 + (VMEM,) * 3,
+        scratch_shapes=[pltpu.VMEM(big.shape, F32)] * 4 + [pltpu.VMEM(wide.shape, F32)] * 3
+        + sems(24) + [pltpu.SemaphoreType.DMA, pltpu.SemaphoreType.DMA((7,))],
         compiler_params=talk(1),
-        name="dispatch",
-    )(packed)
+        name="dispatch_and_scan",
+    )(packed, scan_input, delta_raw, state_input, state_output, log_rates, block_states, skip_gain.reshape(1, 512))
     parts, probes = pl.pallas_call(
         expert_kernel,
         grid=(8,),
@@ -579,59 +662,30 @@
         scratch_shapes=[pltpu.VMEM((TT, 256), BF16)],
         name="resid_and_inner",
     )(expert_ids, expert_route_weights, returned, told, out_grad, out_weight)
-    inner_grad = pl.pallas_call(
-        spread_kernel,
-        out_shape=shape((TT, 512)),
-        in_specs=[VMEM],
-        out_specs=VMEM,
-        scratch_shapes=[pltpu.VMEM((8, 2, 64, 512), BF16)] * 2 + [pltpu.VMEM((8, 32, 512), F32)] * 2
-        + [pltpu.VMEM((4, 64, 512), F32)] * 2 + sems(24),
+    gate_grad, input_grad, delta_grad, rates_grad, skip_grad = pl.pallas_call(
+        tail_kernel,
+        out_shape=(shape((512, 128), BF16),) * 3 + (shape((16, 512)), shape((1, 512))),
+        in_specs=[ANY] * 8 + [VMEM] * 5,
+        out_specs=(VMEM,) * 5,
+        scratch_shapes=[pltpu.VMEM((4, 4, TT, 512), BF16)] + [pltpu.VMEM((8, 2, 64, 512), BF16)] * 2
+        + [pltpu.VMEM((8, 32, 512), F32)] * 2 + [pltpu.VMEM((4, 64, 512), F32)] * 2 + [pltpu.VMEM((TT, 512), F32)]
+        + [pltpu.VMEM(big.shape, F32)] * 4 + [pltpu.VMEM(wide.shape, F32)] * 6
+        + [pltpu.VMEM((ROWS, 128), F32)] + [pltpu.VMEM((7, ROWS, 128), F32)] * 2
+        + [pltpu.VMEM((72, 128), F32)] * 3 + [pltpu.VMEM((3, 72, 128), F32)]
+        + sems(42) + [pltpu.SemaphoreType.DMA((8,))],
         compiler_params=talk(3),
-        name="inner_sum",
-    )(inner_parts)
-    earlier, steps, signal, scan_out = pl.pallas_call(
-        forward_kernel,
-        out_shape=(shape((TT * 64, 128)), shape((TT * 8, 128)), shape((TT * 8, 128)), shape((TT * 8, 128))),
-        in_specs=[VMEM] * 7,
-        out_specs=(VMEM,) * 4,
-        name="scan_forward",
-    )(scan_input, delta_raw, b_rep, c_rep, rates, start, skip)
-    y_grad, gate_grad, pair = pl.pallas_call(
-        middle_kernel,
-        out_shape=(shape((TT * 8, 128)), shape((512, 128), BF16), shape((128, 128))),
-        in_specs=[VMEM] * 6,
-        out_specs=(VMEM,) * 3,
-        name="adjoint_summary",
-    )(inner_grad, mixer_gate_branch, c_rep, rates, steps, scan_out)
-    pairs = pl.pallas_call(
-        gather_kernel,
-        out_shape=shape((8, 128, 128)),
-        in_specs=[VMEM],
-        out_specs=VMEM,
-        scratch_shapes=sems(7) + [pltpu.SemaphoreType.DMA],
-        compiler_params=talk(4),
-        name="carry_gather",
-    )(pair)
-    me = lax.axis_index("seq").astype(jnp.int32).reshape(1)
-    input_grad, delta_grad, part = pl.pallas_call(
-        final_kernel,
-        out_shape=(shape((512, 128), BF16), shape((512, 128), BF16), shape((72, 128))),
-        in_specs=[SMEM] + [VMEM] * 10,
-        out_specs=(VMEM,) * 3,
-        scratch_shapes=[pltpu.VMEM((TT * 8, 128), F32)] * 2,
-        name="adjoint_final",
-    )(me, pairs, y_grad, earlier, steps, signal, delta_raw, b_rep, c_rep, rates, skip)
-    total = pl.pallas_call(
-        total_kernel,
-        out_shape=shape((72, 128)),
-        in_specs=[VMEM],
-        out_specs=VMEM,
-        scratch_shapes=[pltpu.VMEM((8, 72, 128), F32)] + sems(7),
-        compiler_params=talk(5),
-        name="token_sums",
-    )(part)
-    rates_grad = total[:64].reshape(16, 512)
-    skip_grad = total[64:68].reshape(512)
+        name="adjoint_tail",
+    )(inner_parts, saved[0], saved[1], saved[2], saved[3], saved[4], saved[5], saved[6],
+      mixer_gate_branch, delta_raw, rate, decay, skip)
+    results = (gate_grad, input_grad, delta_grad, rates_grad, skip_grad)
+    gate_grad, input_grad, delta_grad, rates_grad, skip_grad = pl.pallas_call(
+        finish_kernel,
+        out_shape=tuple(shape(r.shape, r.dtype) for r in results),
+        in_specs=[VMEM] * 5,
+        out_specs=(VMEM,) * 5,
+        name="finish",
+    )(*results)
+    skip_grad = skip_grad.reshape(512)
     return (resid_grad, probs_grad, input_grad, delta_grad, gate_grad, rates_grad, skip_grad)
 
 

time: 197 us -> 155 us (0.79)
  Pallas kernels: 187 us -> 151 us
  local copies, waits for them, and re-layouts: 8.54 us -> 2.8 us
    pallas_call x7 -> x3, Pallas kernels: 125 us -> 89.3 us  [the longest x1 49.2 us: local(): pl.pallas_call(dispatch_kernel, out_shape=(shape((8, 16, 2, CAP, 256), BF...]
    reshape x4 -> x0, local copies, waits for them, and re-layouts: 3.11 us -> none  [the longest x1 1.26 us: local(): skip_grad = total[64:68].reshape(512)]
where the time goes in v2:
time: 155 us; the launch traced here: 154 us
  Pallas kernels  151 us (97%)
  local copies, waits for them, and re-layouts  2.8 us (2%)
    pallas_call x1, Pallas kernels, local(): pl.pallas_call(dispatch_kernel, out_shape=(shape((8, 16, 2, CAP, 256), BF...  49.2 us
    pallas_call x1, Pallas kernels, local(): pl.pallas_call(tail_kernel, out_shape=(shape((512, 128), BF16),) * 3 + (s...  38.2 us
    pallas_call x1, Pallas kernels, local(): pl.pallas_call(combine_kernel, out_shape=(shape((16, CAP, 256), BF16), sh...  36.3 us
    pallas_call x1, Pallas kernels, local(): pl.pallas_call(expert_kernel, grid=(8,), out_shape=(shape((8, 16, CAP, 25...  17 us
    pallas_call x1, Pallas kernels, local(): pl.pallas_call(resid_kernel, grid=(4,), out_shape=(shape((TT, 256), BF16)...  6.01 us

profile of v2, /device:TPU:1, one launch (start us, length us, event | category | flops | bytes accessed | tf_op | source)
XLA Modules:
  0.0 154.4 jit_solution(10645946536238905604)
XLA Ops:
  0.6 1.4 copy.24.ids_ref
  2.0 2.4 %pack_rows.1.s_ref = bf16[8,2,48,256]{3,2,1,0:T(8,128)(2,1)} custom-call(s32[128,2]{1,0:T(8,128)} %copy.24.ids_ref, bf16[128,256]{1,0:T(8,128)(2,1)} %x_ref.1, bf16[128,256]{1,0:T(8,128)(2,1)} %g_ref.3), custom_call_target="tpu_custom_call" | custom-call | tf_op jit(solution)/shard_map/pack_rows/pallas_call | solution.py:592
  4.4 49.2 %dispatch_and_scan.1 = (bf16[8,16,2,48,256]{4,3,2,1,0:T(8,128)(2,1)}, f32[8192,128]{1,0:T(8,128)}, f32[8192,128]{1,0:T(8,128)}, f32[8192,128]{1,0:T(8,128)}, f32...) custom-call(bf16[8,2,48,256]{3,2,1,0:T(8,128)(2,1)} %pack_rows.1.s_r, ...), custom_call_target="tpu_custom_call" | custom-call | tf_op jit(solution)/shard_map/dispatch_and_scan/pallas_call | solution.py:601
  53.6 0.0 copy-start.1
  53.7 17.0 %experts.1 = (bf16[8,16,48,256]{3,2,1,0:T(8,128)(2,1)}, f32[8,384]{1,0:T(8,128)}) custom-call(bf16[8,16,2,48,256]{4,3,2,1,0:T(8,128)(2,1)} %get-tuple-element.35.r_ref, bf16[1,4096,512]{2,1,0:T(8,128)(2,1)} %wg_ref.1, bf16[1,4096,512]{2,1,0:T(8,128)(2,1)} %wu_ref.1, bf16[1,512,4096]{2,1,0:T(8,128)(2,1)} %wd_ref.1), custom_call_target="tpu_custom_call" | custom-call | tf_op jit(solution)/shard_map/experts/pallas_call | solution.py:612
  70.7 36.3 %combine.1 = (bf16[16,48,256]{2,1,0:T(8,128)(2,1)}, f32[16,8,128]{2,1,0:T(8,128)}) custom-call(bf16[8,16,48,256]{3,2,1,0:T(8,128)(2,1)} %get-tuple-element.36.p_ref, f32[8,384]{1,0:T(8,128)} %get-tuple-element.37.pr_ref), custom_call_target="tpu_custom_call" | custom-call | tf_op jit(solution)/shard_map/combine/pallas_call | solution.py:629
  106.9 0.0 copy-done.1
  106.9 0.7 copy.25.w_ref
  107.7 6.0 %resid_and_inner.1 = (bf16[128,256]{1,0:T(8,128)(2,1)}, f32[128,2]{1,0:T(8,128)}, bf16[4,4,128,512]{3,2,1,0:T(8,128)(2,1)}) custom-call(s32[128,2]{1,0:T(8,128)} %copy.24.ids_ref, f32[128,2]{1,0:T(8,128)} %copy.25.w_ref, bf16[16,48,256]{2,1,0:T(8,128)(2,1)} %get-tuple-element.38.t_ref, f32[16,8,128]{2,1,0:T(8,128)} %get-tuple-element.39.tp_ref, ...), custom_call_target="tpu_custom_call" | custom-call | tf_op jit(solution)/shard_map/resid_and_inner/pallas_call | solution.py:645
  113.7 0.0 copy-start
  113.7 38.2 %adjoint_tail.1 = (bf16[512,128]{1,0:T(8,128)(2,1)}, bf16[512,128]{1,0:T(8,128)(2,1)}, bf16[512,128]{1,0:T(8,128)(2,1)}, f32[16,512]{1,0:T(8,128)}, f32[1,512]{1,0:T(1,128)}) custom-call(bf16[4,4,128,512]{3,2,1,0:T(8,128)(2,1)} %get-tuple-element.42.i_ref, f32[8192,128]{1,0:T(8,128)} %get-tuple-element.43.a_h, f32[8192,128]{1,0:T(8,128)} %get-tuple-element.44.ear_h, ...), custom_call_target="tpu_custom_call" | custom-call | tf_op jit(solution)/shard_map/adjoint_tail/pallas_call | solution.py:665
  151.9 1.8 %finish.1 = (bf16[512,128]{1,0:T(8,128)(2,1)}, bf16[512,128]{1,0:T(8,128)(2,1)}, bf16[512,128]{1,0:T(8,128)(2,1)}, f32[16,512]{1,0:T(8,128)}, f32[1,512]{1,0:T(1,128)}) custom-call(bf16[512,128]{1,0:T(8,128)(2,1)} %get-tuple-element.53.refs_0_, bf16[512,128]{1,0:T(8,128)(2,1)} %get-tuple-element.54.refs_1_, bf16[512,128]{1,0:T(8,128)(2,1)} %get-tuple-element.55.refs_2_, ...), custom_call_target="tpu_custom_call" | custom-call | tf_op jit(solution)/shard_map/finish/pallas_call | solution.py:681
  153.7 0.0 copy-done
  153.7 0.6 copy.26
Async XLA Ops:
  53.6 53.3 %copy-start.1 = (f32[128,2]{0,1:T(2,128)S(1)}, f32[128,2]{0,1:T(2,128)}, u32[]{:S(2)}) copy-start(f32[128,2]{0,1:T(2,128)} %param.19) | copy-start | bytes 3076
  113.7 40.0 %copy-start = (f32[128,2]{1,0:T(8,128)S(1)}, f32[128,2]{1,0:T(8,128)}, u32[]{:S(2)}) copy-start(f32[128,2]{1,0:T(8,128)} %get-tuple-element.64) | copy-start | bytes 3076
